TPU v7x, 512 devices: a whole 4x4x16 slice. The times are simulated.
512 devices in a mesh: seq: 16 (over z), head: 32 (over x, y, core).
Axes of the slice: x: 4, y: 4, z: 16, core: 2. Of those that a mesh axis runs over, the one named last changes fastest.
Arguments:
- queries: bfloat16 [16384, 8192], P('seq', 'head'), may hold values from -6 to 6
- keys: bfloat16 [16384, 8192], P('seq', 'head'), may hold values from -1 to 1
- values: bfloat16 [16384, 8192], P('seq', 'head'), may hold values from -40 to 40
- log_decay: float32 [64, 16384], P('head', 'seq'), may hold values from -1 to 0
- gain: float32 [8192], P('head'), may hold values from 0.25 to 1.75
- out_grad: bfloat16 [16384, 8192], P('seq', 'head'), may hold values from -16 to 16
Outputs:
- output: bfloat16 [16384, 8192], P('seq', 'head')
- query_grad: bfloat16 [16384, 8192], P('seq', 'head')
- key_grad: bfloat16 [16384, 8192], P('seq', 'head')
- value_grad: bfloat16 [16384, 8192], P('seq', 'head')
- gain_grad: float32 [8192], P('head')
All inputs are finite; a program needn't handle non-finite values.
Results may differ from a plain program's by a relative error of at most 0.001.
Values sent between devices are 32-bit elements; how exact they have to be, the bound alone decides.
No kernel may reach another device: no remote copies, remote signals or barrier semaphores. Data moves between devices by JAX's collectives and lax.ppermute only.
A program may use at most 64 MiB of HBM per device.

v0:
```python
import jax
import jax.numpy as jnp
from jax import lax
from jax.sharding import PartitionSpec as P

epsilon = 1e-06
highest = lax.Precision.HIGHEST


def passed_along(value, axis, steps):
    count = lax.axis_size(axis)
    initial, last = (max(0, -steps), min(count, count - steps))
    return lax.ppermute(value, axis, [(source, source + steps) for source in range(initial, last)])


def to_blocks(matrix, heads_local, block_count, block_rows):
    head_width = matrix.shape[1] // heads_local
    return matrix.reshape(block_count, block_rows, heads_local, head_width).transpose(2, 0, 1, 3)


def from_blocks(blocked):
    heads_local, block_count, block_rows, head_width = blocked.shape
    return blocked.transpose(1, 2, 0, 3).reshape(block_count * block_rows, heads_local * head_width)


def carry_forward(device_decay, device_state):

    def relay_step(iteration, prefix):
        outgoing = jnp.exp(device_decay)[:, None, None] * prefix + device_state
        return passed_along(outgoing, "seq", 1)

    return lax.fori_loop(0, lax.axis_size("seq") - 1, relay_step, jnp.zeros_like(device_state))


def carry_backward(device_decay, device_back):

    def relay_step(iteration, suffix):
        outgoing = jnp.exp(device_decay)[:, None, None] * suffix + device_back
        return passed_along(outgoing, "seq", -1)

    return lax.fori_loop(0, lax.axis_size("seq") - 1, relay_step, jnp.zeros_like(device_back))


def local(queries, keys, values, log_decay, gain, out_grad):
    token_rows, channels = queries.shape
    heads_local = log_decay.shape[0]
    block_rows = min(256, token_rows)
    block_count = token_rows // block_rows
    total_channels = channels * lax.axis_size("head")
    query_narrow = to_blocks(queries, heads_local, block_count, block_rows)
    key_narrow = to_blocks(keys, heads_local, block_count, block_rows)
    query_blocks = query_narrow.astype(jnp.float32)
    key_blocks = key_narrow.astype(jnp.float32)
    value_blocks = to_blocks(values, heads_local, block_count, block_rows).astype(jnp.float32)
    decay_sum = jnp.cumsum(log_decay.reshape(heads_local, block_count, block_rows), axis=2)
    block_total = decay_sum[:, :, -1]
    causal = jnp.arange(block_rows)[:, None] >= jnp.arange(block_rows)[None, :]
    mask_decay = jnp.exp(
        jnp.where(causal, decay_sum[..., :, None] - decay_sum[..., None, :], -1e30)
    )
    from_start = jnp.exp(decay_sum)[..., None]
    to_end = jnp.exp(block_total[..., None] - decay_sum)[..., None]
    scores = (
        jnp.einsum("hnid,hnjd->hnij", query_narrow, key_narrow, preferred_element_type=jnp.float32)
        * mask_decay
    )
    inside = jnp.einsum("hnij,hnjd->hnid", scores, value_blocks, precision=highest)
    own_states = jnp.einsum("hnjd,hnje->hnde", key_blocks * to_end, value_blocks, precision=highest)
    device_decay = jnp.sum(block_total, axis=1)
    device_state = jnp.zeros_like(own_states[:, 0])
    for block_index in range(block_count):
        device_state = (
            jnp.exp(block_total[:, block_index])[:, None, None] * device_state
            + own_states[:, block_index]
        )
    incoming = carry_forward(device_decay, device_state)
    entering = []
    running = incoming
    for block_index in range(block_count):
        entering.append(running)
        running = (
            jnp.exp(block_total[:, block_index])[:, None, None] * running
            + own_states[:, block_index]
        )
    entering = jnp.stack(entering, axis=1)
    attended = inside + from_start * jnp.einsum(
        "hnid,hnde->hnie", query_blocks, entering, precision=highest
    )
    flattened = from_blocks(attended)
    grad_wide = out_grad.astype(jnp.float32)
    normed_grad = grad_wide * gain
    squares = lax.psum(jnp.sum(flattened * flattened, axis=1), "head")
    inverse = 1.0 / jnp.sqrt(squares / total_channels + epsilon)
    normed = flattened * inverse[:, None]
    projected = lax.psum(jnp.sum(normed_grad * normed, axis=1), "head")
    output = (normed * gain).astype(jnp.bfloat16)
    gain_part = jnp.sum(grad_wide * normed, axis=0)
    flat_grad = (normed_grad - normed * (projected / total_channels)[:, None]) * inverse[:, None]
    attended_grad = to_blocks(flat_grad, heads_local, block_count, block_rows)
    score_grad = (
        jnp.einsum("hnid,hnjd->hnij", attended_grad, value_blocks, precision=highest) * mask_decay
    )
    query_grad = jnp.einsum("hnij,hnjd->hnid", score_grad, key_blocks, precision=highest)
    query_grad = query_grad + from_start * jnp.einsum(
        "hnie,hnde->hnid", attended_grad, entering, precision=highest
    )
    key_grad = jnp.einsum("hnij,hnid->hnjd", score_grad, query_blocks, precision=highest)
    value_grad = jnp.einsum("hnij,hnid->hnjd", scores, attended_grad, precision=highest)
    own_back = jnp.einsum(
        "hnid,hnie->hnde", query_blocks * from_start, attended_grad, precision=highest
    )
    device_back = jnp.zeros_like(device_state)
    for block_index in reversed(range(block_count)):
        device_back = (
            own_back[:, block_index]
            + jnp.exp(block_total[:, block_index])[:, None, None] * device_back
        )
    later_sum = carry_backward(device_decay, device_back)
    leaving = []
    running = later_sum
    for block_index in reversed(range(block_count)):
        leaving.append(running)
        running = (
            own_back[:, block_index] + jnp.exp(block_total[:, block_index])[:, None, None] * running
        )
    leaving = jnp.stack(leaving[::-1], axis=1)
    key_grad = key_grad + to_end * jnp.einsum(
        "hnje,hnde->hnjd", value_blocks, leaving, precision=highest
    )
    value_grad = value_grad + to_end * jnp.einsum(
        "hnjd,hnde->hnje", key_blocks, leaving, precision=highest
    )
    gain_grad = lax.psum(gain_part, "seq")
    return (
        output,
        from_blocks(query_grad).astype(jnp.bfloat16),
        from_blocks(key_grad).astype(jnp.bfloat16),
        from_blocks(value_grad).astype(jnp.bfloat16),
        gain_grad,
    )


def solution(mesh):
    in_specs = (
        P("seq", "head"),
        P("seq", "head"),
        P("seq", "head"),
        P("head", "seq"),
        P("head"),
        P("seq", "head"),
    )
    out_specs = (P("seq", "head"), P("seq", "head"), P("seq", "head"), P("seq", "head"), P("head"))
    return jax.shard_map(local, mesh=mesh, in_specs=in_specs, out_specs=out_specs, check_vma=False)
```

profile of v0, /device:TPU:96, one launch (start us, length us, event | category | flops | bytes accessed | tf_op | source)
XLA Modules:
  0.0 471.4 jit_solution(15646903390274113141)
XLA Ops:
  1.3 2.4 reduce-window.6
  9.9 125.4 %while.24 = (s32[]{:T(128)}, f32[2,128,128]{2,1,0:T(8,128)S(1)}, f32[2,1,1]{0,2,1:T(1,128)S(1)}, f32[2,128,128]{2,1,0:T(8,128)S(1)}, s32[]{:T(128)}) while((s32[]{:T(128)}, f32[2,128,128]{2,1,0:T(8,128)S(1)}, f32[2,1,1]{0,2,1:T(1,128)S(1)}, f32[2,128,128]{2,1,0:T(8,128)S(1)}, s32[]{:T(128)}) %tuple.63), condition=%wide.region_4.5_spmd, body=%wide.region_3.4_spmd.sunk | while | flops 65538 | bytes 917613 | solution.py:32
  10.0 5.0 %collective-permute-start = (f32[2,128,128]{2,1,0:T(8,128)S(1)}, f32[2,128,128]{2,1,0:T(8,128)S(1)}, u32[]{:S(2)}, u32[]{:S(2)}) collective-permute-start(f32[2,128,128]{2,1,0:T(8,128)S(1)} %multiply_add_fusion.10), channel_id=1, source_target_pairs={{0,32},{32,64},{64,96},{96,128},{128,160},{160,192},{192,224},{224... | collective-permute-start | bytes 393224 | tf_op jit(solution)/shard_map/while/body/eval_jaxpr/ppermute | solution.py:13
  15.0 2.7 collective-permute-done
  17.8 5.6 %collective-permute-start = (f32[2,128,128]{2,1,0:T(8,128)S(1)}, f32[2,128,128]{2,1,0:T(8,128)S(1)}, u32[]{:S(2)}, u32[]{:S(2)}) collective-permute-start(f32[2,128,128]{2,1,0:T(8,128)S(1)} %multiply_add_fusion.10), channel_id=1, source_target_pairs={{0,32},{32,64},{64,96},{96,128},{128,160},{160,192},{192,224},{224... | collective-permute-start | bytes 393224 | tf_op jit(solution)/shard_map/while/body/eval_jaxpr/ppermute | solution.py:13
  23.5 2.5 collective-permute-done
  26.0 5.6 %collective-permute-start = (f32[2,128,128]{2,1,0:T(8,128)S(1)}, f32[2,128,128]{2,1,0:T(8,128)S(1)}, u32[]{:S(2)}, u32[]{:S(2)}) collective-permute-start(f32[2,128,128]{2,1,0:T(8,128)S(1)} %multiply_add_fusion.10), channel_id=1, source_target_pairs={{0,32},{32,64},{64,96},{96,128},{128,160},{160,192},{192,224},{224... | collective-permute-start | bytes 393224 | tf_op jit(solution)/shard_map/while/body/eval_jaxpr/ppermute | solution.py:13
  31.6 2.5 collective-permute-done
  34.2 5.6 %collective-permute-start = (f32[2,128,128]{2,1,0:T(8,128)S(1)}, f32[2,128,128]{2,1,0:T(8,128)S(1)}, u32[]{:S(2)}, u32[]{:S(2)}) collective-permute-start(f32[2,128,128]{2,1,0:T(8,128)S(1)} %multiply_add_fusion.10), channel_id=1, source_target_pairs={{0,32},{32,64},{64,96},{96,128},{128,160},{160,192},{192,224},{224... | collective-permute-start | bytes 393224 | tf_op jit(solution)/shard_map/while/body/eval_jaxpr/ppermute | solution.py:13
  39.8 2.5 collective-permute-done
  42.3 5.6 %collective-permute-start = (f32[2,128,128]{2,1,0:T(8,128)S(1)}, f32[2,128,128]{2,1,0:T(8,128)S(1)}, u32[]{:S(2)}, u32[]{:S(2)}) collective-permute-start(f32[2,128,128]{2,1,0:T(8,128)S(1)} %multiply_add_fusion.10), channel_id=1, source_target_pairs={{0,32},{32,64},{64,96},{96,128},{128,160},{160,192},{192,224},{224... | collective-permute-start | bytes 393224 | tf_op jit(solution)/shard_map/while/body/eval_jaxpr/ppermute | solution.py:13
  47.9 2.5 collective-permute-done
  50.5 5.6 %collective-permute-start = (f32[2,128,128]{2,1,0:T(8,128)S(1)}, f32[2,128,128]{2,1,0:T(8,128)S(1)}, u32[]{:S(2)}, u32[]{:S(2)}) collective-permute-start(f32[2,128,128]{2,1,0:T(8,128)S(1)} %multiply_add_fusion.10), channel_id=1, source_target_pairs={{0,32},{32,64},{64,96},{96,128},{128,160},{160,192},{192,224},{224... | collective-permute-start | bytes 393224 | tf_op jit(solution)/shard_map/while/body/eval_jaxpr/ppermute | solution.py:13
  56.1 3.4 collective-permute-done
  59.6 5.6 %collective-permute-start = (f32[2,128,128]{2,1,0:T(8,128)S(1)}, f32[2,128,128]{2,1,0:T(8,128)S(1)}, u32[]{:S(2)}, u32[]{:S(2)}) collective-permute-start(f32[2,128,128]{2,1,0:T(8,128)S(1)} %multiply_add_fusion.10), channel_id=1, source_target_pairs={{0,32},{32,64},{64,96},{96,128},{128,160},{160,192},{192,224},{224... | collective-permute-start | bytes 393224 | tf_op jit(solution)/shard_map/while/body/eval_jaxpr/ppermute | solution.py:13
  65.2 3.1 collective-permute-done
  68.4 5.6 %collective-permute-start = (f32[2,128,128]{2,1,0:T(8,128)S(1)}, f32[2,128,128]{2,1,0:T(8,128)S(1)}, u32[]{:S(2)}, u32[]{:S(2)}) collective-permute-start(f32[2,128,128]{2,1,0:T(8,128)S(1)} %multiply_add_fusion.10), channel_id=1, source_target_pairs={{0,32},{32,64},{64,96},{96,128},{128,160},{160,192},{192,224},{224... | collective-permute-start | bytes 393224 | tf_op jit(solution)/shard_map/while/body/eval_jaxpr/ppermute | solution.py:13
  74.1 2.5 collective-permute-done
  76.6 5.6 %collective-permute-start = (f32[2,128,128]{2,1,0:T(8,128)S(1)}, f32[2,128,128]{2,1,0:T(8,128)S(1)}, u32[]{:S(2)}, u32[]{:S(2)}) collective-permute-start(f32[2,128,128]{2,1,0:T(8,128)S(1)} %multiply_add_fusion.10), channel_id=1, source_target_pairs={{0,32},{32,64},{64,96},{96,128},{128,160},{160,192},{192,224},{224... | collective-permute-start | bytes 393224 | tf_op jit(solution)/shard_map/while/body/eval_jaxpr/ppermute | solution.py:13
  82.2 2.5 collective-permute-done
  84.8 5.6 %collective-permute-start = (f32[2,128,128]{2,1,0:T(8,128)S(1)}, f32[2,128,128]{2,1,0:T(8,128)S(1)}, u32[]{:S(2)}, u32[]{:S(2)}) collective-permute-start(f32[2,128,128]{2,1,0:T(8,128)S(1)} %multiply_add_fusion.10), channel_id=1, source_target_pairs={{0,32},{32,64},{64,96},{96,128},{128,160},{160,192},{192,224},{224... | collective-permute-start | bytes 393224 | tf_op jit(solution)/shard_map/while/body/eval_jaxpr/ppermute | solution.py:13
  90.4 2.5 collective-permute-done
  92.9 5.6 %collective-permute-start = (f32[2,128,128]{2,1,0:T(8,128)S(1)}, f32[2,128,128]{2,1,0:T(8,128)S(1)}, u32[]{:S(2)}, u32[]{:S(2)}) collective-permute-start(f32[2,128,128]{2,1,0:T(8,128)S(1)} %multiply_add_fusion.10), channel_id=1, source_target_pairs={{0,32},{32,64},{64,96},{96,128},{128,160},{160,192},{192,224},{224... | collective-permute-start | bytes 393224 | tf_op jit(solution)/shard_map/while/body/eval_jaxpr/ppermute | solution.py:13
  98.5 2.5 collective-permute-done
  101.1 5.6 %collective-permute-start = (f32[2,128,128]{2,1,0:T(8,128)S(1)}, f32[2,128,128]{2,1,0:T(8,128)S(1)}, u32[]{:S(2)}, u32[]{:S(2)}) collective-permute-start(f32[2,128,128]{2,1,0:T(8,128)S(1)} %multiply_add_fusion.10), channel_id=1, source_target_pairs={{0,32},{32,64},{64,96},{96,128},{128,160},{160,192},{192,224},{224... | collective-permute-start | bytes 393224 | tf_op jit(solution)/shard_map/while/body/eval_jaxpr/ppermute | solution.py:13
  106.7 3.0 collective-permute-done
  109.8 5.6 %collective-permute-start = (f32[2,128,128]{2,1,0:T(8,128)S(1)}, f32[2,128,128]{2,1,0:T(8,128)S(1)}, u32[]{:S(2)}, u32[]{:S(2)}) collective-permute-start(f32[2,128,128]{2,1,0:T(8,128)S(1)} %multiply_add_fusion.10), channel_id=1, source_target_pairs={{0,32},{32,64},{64,96},{96,128},{128,160},{160,192},{192,224},{224... | collective-permute-start | bytes 393224 | tf_op jit(solution)/shard_map/while/body/eval_jaxpr/ppermute | solution.py:13
  115.4 3.5 collective-permute-done
  119.0 5.6 %collective-permute-start = (f32[2,128,128]{2,1,0:T(8,128)S(1)}, f32[2,128,128]{2,1,0:T(8,128)S(1)}, u32[]{:S(2)}, u32[]{:S(2)}) collective-permute-start(f32[2,128,128]{2,1,0:T(8,128)S(1)} %multiply_add_fusion.10), channel_id=1, source_target_pairs={{0,32},{32,64},{64,96},{96,128},{128,160},{160,192},{192,224},{224... | collective-permute-start | bytes 393224 | tf_op jit(solution)/shard_map/while/body/eval_jaxpr/ppermute | solution.py:13
  124.6 2.5 collective-permute-done
  127.2 5.6 %collective-permute-start = (f32[2,128,128]{2,1,0:T(8,128)S(1)}, f32[2,128,128]{2,1,0:T(8,128)S(1)}, u32[]{:S(2)}, u32[]{:S(2)}) collective-permute-start(f32[2,128,128]{2,1,0:T(8,128)S(1)} %multiply_add_fusion.10), channel_id=1, source_target_pairs={{0,32},{32,64},{64,96},{96,128},{128,160},{160,192},{192,224},{224... | collective-permute-start | bytes 393224 | tf_op jit(solution)/shard_map/while/body/eval_jaxpr/ppermute | solution.py:13
  132.8 2.5 collective-permute-done
  139.9 62.7 %psum.21 = f32[1024]{0:T(1024)S(1)} all-reduce(f32[1024]{0:T(1024)S(1)} %bitcast.231), channel_id=1, replica_groups=mesh['seq'=16,'head'=32] {'head'}, use_global_device_ids=true, to_apply=%region_6.7 | all-reduce | flops 1024 | bytes 8192 | tf_op jit(solution)/shard_map/psum | solution.py:92
  204.7 32.4 %psum.23 = f32[256]{0:T(256)} all-reduce(f32[256]{0:T(256)S(1)} %get-tuple-element.107), channel_id=1, replica_groups=mesh['seq'=16,'head'=32] {'seq'}, use_global_device_ids=true, to_apply=%region_12.13 | all-reduce | flops 256 | bytes 2048 | tf_op jit(solution)/shard_map/psum | solution.py:133
  237.2 62.7 %psum.22 = f32[1024]{0:T(1024)S(1)} all-reduce(f32[1024]{0:T(1024)S(1)} %get-tuple-element.108), channel_id=1, replica_groups=mesh['seq'=16,'head'=32] {'head'}, use_global_device_ids=true, to_apply=%region_8.9 | all-reduce | flops 1024 | bytes 8192 | tf_op jit(solution)/shard_map/psum | solution.py:95
  303.1 6.1 %convolution_bitcast_fusion.4 = f32[4,256,2,128]{3,1,0,2:T(8,128)} fusion(f32[2,4,256,256]{3,2,1,0:T(8,128)} %copy-done, f32[4,256,2,128]{3,2,1,0:T(2,128)S(1)} %reshape.129), kind=kOutput, calls=%fused_computation.11 | convolution fusion | flops 805306368 | bytes 4194304 | tf_op jit(solution)/shard_map/hnij,hnid->hnjd/dot_general | solution.py:108
  310.5 147.5 %while.25 = (s32[]{:T(128)}, f32[2,128,128]{2,1,0:T(8,128)S(1)}, f32[2,1,1]{0,2,1:T(1,128)}, f32[2,128,128]{2,1,0:T(8,128)S(1)}, s32[]{:T(128)}) while((s32[]{:T(128)}, f32[2,128,128]{2,1,0:T(8,128)S(1)}, f32[2,1,1]{0,2,1:T(1,128)}, f32[2,128,128]{2,1,0:T(8,128)S(1)}, s32[]{:T(128)}) %tuple.69), condition=%wide.region_10.11_spmd, body=%wide.region_9.10_spmd.sunk | while | flops 65538 | bytes 917613 | solution.py:41
  312.1 1.9 collective-permute-start.1
  314.1 6.6 %collective-permute-done.1 = f32[2,128,128]{2,1,0:T(8,128)S(1)} collective-permute-done((f32[2,128,128]{2,1,0:T(8,128)}, f32[2,128,128]{2,1,0:T(8,128)S(1)}, u32[]{:S(2)}, u32[]{:S(2)}) %collective-permute-start.1) | collective-permute-done | bytes 131104 | tf_op jit(solution)/shard_map/while/body/eval_jaxpr/ppermute | solution.py:13
  322.1 1.9 collective-permute-start.1
  324.0 6.4 %collective-permute-done.1 = f32[2,128,128]{2,1,0:T(8,128)S(1)} collective-permute-done((f32[2,128,128]{2,1,0:T(8,128)}, f32[2,128,128]{2,1,0:T(8,128)S(1)}, u32[]{:S(2)}, u32[]{:S(2)}) %collective-permute-start.1) | collective-permute-done | bytes 131104 | tf_op jit(solution)/shard_map/while/body/eval_jaxpr/ppermute | solution.py:13
  331.8 1.9 collective-permute-start.1
  333.7 6.4 %collective-permute-done.1 = f32[2,128,128]{2,1,0:T(8,128)S(1)} collective-permute-done((f32[2,128,128]{2,1,0:T(8,128)}, f32[2,128,128]{2,1,0:T(8,128)S(1)}, u32[]{:S(2)}, u32[]{:S(2)}) %collective-permute-start.1) | collective-permute-done | bytes 131104 | tf_op jit(solution)/shard_map/while/body/eval_jaxpr/ppermute | solution.py:13
  341.5 1.9 collective-permute-start.1
  343.4 6.4 %collective-permute-done.1 = f32[2,128,128]{2,1,0:T(8,128)S(1)} collective-permute-done((f32[2,128,128]{2,1,0:T(8,128)}, f32[2,128,128]{2,1,0:T(8,128)S(1)}, u32[]{:S(2)}, u32[]{:S(2)}) %collective-permute-start.1) | collective-permute-done | bytes 131104 | tf_op jit(solution)/shard_map/while/body/eval_jaxpr/ppermute | solution.py:13
  351.2 1.9 collective-permute-start.1
  353.1 6.4 %collective-permute-done.1 = f32[2,128,128]{2,1,0:T(8,128)S(1)} collective-permute-done((f32[2,128,128]{2,1,0:T(8,128)}, f32[2,128,128]{2,1,0:T(8,128)S(1)}, u32[]{:S(2)}, u32[]{:S(2)}) %collective-permute-start.1) | collective-permute-done | bytes 131104 | tf_op jit(solution)/shard_map/while/body/eval_jaxpr/ppermute | solution.py:13
  360.8 1.9 collective-permute-start.1
  362.8 6.4 %collective-permute-done.1 = f32[2,128,128]{2,1,0:T(8,128)S(1)} collective-permute-done((f32[2,128,128]{2,1,0:T(8,128)}, f32[2,128,128]{2,1,0:T(8,128)S(1)}, u32[]{:S(2)}, u32[]{:S(2)}) %collective-permute-start.1) | collective-permute-done | bytes 131104 | tf_op jit(solution)/shard_map/while/body/eval_jaxpr/ppermute | solution.py:13
  370.5 1.9 collective-permute-start.1
  372.4 6.9 %collective-permute-done.1 = f32[2,128,128]{2,1,0:T(8,128)S(1)} collective-permute-done((f32[2,128,128]{2,1,0:T(8,128)}, f32[2,128,128]{2,1,0:T(8,128)S(1)}, u32[]{:S(2)}, u32[]{:S(2)}) %collective-permute-start.1) | collective-permute-done | bytes 131104 | tf_op jit(solution)/shard_map/while/body/eval_jaxpr/ppermute | solution.py:13
  382.7 7.4 %collective-permute-done.1 = f32[2,128,128]{2,1,0:T(8,128)S(1)} collective-permute-done((f32[2,128,128]{2,1,0:T(8,128)}, f32[2,128,128]{2,1,0:T(8,128)S(1)}, u32[]{:S(2)}, u32[]{:S(2)}) %collective-permute-start.1) | collective-permute-done | bytes 131104 | tf_op jit(solution)/shard_map/while/body/eval_jaxpr/ppermute | solution.py:13
  393.4 6.6 %collective-permute-done.1 = f32[2,128,128]{2,1,0:T(8,128)S(1)} collective-permute-done((f32[2,128,128]{2,1,0:T(8,128)}, f32[2,128,128]{2,1,0:T(8,128)S(1)}, u32[]{:S(2)}, u32[]{:S(2)}) %collective-permute-start.1) | collective-permute-done | bytes 131104 | tf_op jit(solution)/shard_map/while/body/eval_jaxpr/ppermute | solution.py:13
  401.4 1.9 collective-permute-start.1
  403.3 6.4 %collective-permute-done.1 = f32[2,128,128]{2,1,0:T(8,128)S(1)} collective-permute-done((f32[2,128,128]{2,1,0:T(8,128)}, f32[2,128,128]{2,1,0:T(8,128)S(1)}, u32[]{:S(2)}, u32[]{:S(2)}) %collective-permute-start.1) | collective-permute-done | bytes 131104 | tf_op jit(solution)/shard_map/while/body/eval_jaxpr/ppermute | solution.py:13
  411.1 1.9 collective-permute-start.1
  413.0 6.4 %collective-permute-done.1 = f32[2,128,128]{2,1,0:T(8,128)S(1)} collective-permute-done((f32[2,128,128]{2,1,0:T(8,128)}, f32[2,128,128]{2,1,0:T(8,128)S(1)}, u32[]{:S(2)}, u32[]{:S(2)}) %collective-permute-start.1) | collective-permute-done | bytes 131104 | tf_op jit(solution)/shard_map/while/body/eval_jaxpr/ppermute | solution.py:13
  422.7 6.4 %collective-permute-done.1 = f32[2,128,128]{2,1,0:T(8,128)S(1)} collective-permute-done((f32[2,128,128]{2,1,0:T(8,128)}, f32[2,128,128]{2,1,0:T(8,128)S(1)}, u32[]{:S(2)}, u32[]{:S(2)}) %collective-permute-start.1) | collective-permute-done | bytes 131104 | tf_op jit(solution)/shard_map/while/body/eval_jaxpr/ppermute | solution.py:13
  430.5 1.9 collective-permute-start.1
  432.4 6.4 %collective-permute-done.1 = f32[2,128,128]{2,1,0:T(8,128)S(1)} collective-permute-done((f32[2,128,128]{2,1,0:T(8,128)}, f32[2,128,128]{2,1,0:T(8,128)S(1)}, u32[]{:S(2)}, u32[]{:S(2)}) %collective-permute-start.1) | collective-permute-done | bytes 131104 | tf_op jit(solution)/shard_map/while/body/eval_jaxpr/ppermute | solution.py:13
  440.1 1.9 collective-permute-start.1
  442.1 6.4 %collective-permute-done.1 = f32[2,128,128]{2,1,0:T(8,128)S(1)} collective-permute-done((f32[2,128,128]{2,1,0:T(8,128)}, f32[2,128,128]{2,1,0:T(8,128)S(1)}, u32[]{:S(2)}, u32[]{:S(2)}) %collective-permute-start.1) | collective-permute-done | bytes 131104 | tf_op jit(solution)/shard_map/while/body/eval_jaxpr/ppermute | solution.py:13
  449.8 1.9 collective-permute-start.1
  451.7 6.4 %collective-permute-done.1 = f32[2,128,128]{2,1,0:T(8,128)S(1)} collective-permute-done((f32[2,128,128]{2,1,0:T(8,128)}, f32[2,128,128]{2,1,0:T(8,128)S(1)}, u32[]{:S(2)}, u32[]{:S(2)}) %collective-permute-start.1) | collective-permute-done | bytes 131104 | tf_op jit(solution)/shard_map/while/body/eval_jaxpr/ppermute | solution.py:13
  (130 shorter events, 59.1 us)
Async XLA Ops:
  4.7 5.0 %copy-start.19 = (f32[2]{0:T(128)}, f32[2]{0:T(128)S(1)}, u32[]{:S(2)}) copy-start(f32[2]{0:T(128)S(1)} %get-tuple-element.109) | copy-start | bytes 28
  4.7 130.6 %copy-start.15 = (f32[2]{0:T(128)}, f32[2]{0:T(128)S(1)}, u32[]{:S(2)}) copy-start(f32[2]{0:T(128)S(1)} %get-tuple-element.111) | copy-start | bytes 28
  4.7 130.6 %copy-start.17 = (f32[2]{0:T(128)}, f32[2]{0:T(128)S(1)}, u32[]{:S(2)}) copy-start(f32[2]{0:T(128)S(1)} %get-tuple-element.112) | copy-start | bytes 28
  4.8 130.6 %copy-start.20 = (f32[2]{0:T(128)}, f32[2]{0:T(128)S(1)}, u32[]{:S(2)}) copy-start(f32[2]{0:T(128)S(1)} %get-tuple-element.110) | copy-start | bytes 28
  6.0 3.8 copy-start.11
  6.0 130.0 %copy-start.9 = (pred[256,256]{1,0:T(8,128)(4,1)}, pred[256,256]{1,0:T(8,128)(4,1)S(1)}, u32[]{:S(2)}) copy-start(pred[256,256]{1,0:T(8,128)(4,1)S(1)} %iota_compare_fusion) | copy-start | bytes 196612
  9.7 125.7 %copy-start.8 = (bf16[1024,256]{1,0:T(8,128)(2,1)S(1)}, bf16[1024,256]{1,0:T(8,128)(2,1)}, u32[]{:S(2)}) copy-start(bf16[1024,256]{1,0:T(8,128)(2,1)} %param.10) | copy-start | bytes 1572868
  10.0 7.8 %collective-permute-start = (f32[2,128,128]{2,1,0:T(8,128)S(1)}, f32[2,128,128]{2,1,0:T(8,128)S(1)}, u32[]{:S(2)}, u32[]{:S(2)}) collective-permute-start(f32[2,128,128]{2,1,0:T(8,128)S(1)} %multiply_add_fusion.10), channel_id=1, source_target_pairs={{0,32},{32,64},{64,96},{96,128},{128,160},{160,192},{192,224},{224... | collective-permute-start | bytes 393224 | tf_op jit(solution)/shard_map/while/body/eval_jaxpr/ppermute | solution.py:13
  17.8 8.1 %collective-permute-start = (f32[2,128,128]{2,1,0:T(8,128)S(1)}, f32[2,128,128]{2,1,0:T(8,128)S(1)}, u32[]{:S(2)}, u32[]{:S(2)}) collective-permute-start(f32[2,128,128]{2,1,0:T(8,128)S(1)} %multiply_add_fusion.10), channel_id=1, source_target_pairs={{0,32},{32,64},{64,96},{96,128},{128,160},{160,192},{192,224},{224... | collective-permute-start | bytes 393224 | tf_op jit(solution)/shard_map/while/body/eval_jaxpr/ppermute | solution.py:13
  26.0 8.1 %collective-permute-start = (f32[2,128,128]{2,1,0:T(8,128)S(1)}, f32[2,128,128]{2,1,0:T(8,128)S(1)}, u32[]{:S(2)}, u32[]{:S(2)}) collective-permute-start(f32[2,128,128]{2,1,0:T(8,128)S(1)} %multiply_add_fusion.10), channel_id=1, source_target_pairs={{0,32},{32,64},{64,96},{96,128},{128,160},{160,192},{192,224},{224... | collective-permute-start | bytes 393224 | tf_op jit(solution)/shard_map/while/body/eval_jaxpr/ppermute | solution.py:13
  34.2 8.1 %collective-permute-start = (f32[2,128,128]{2,1,0:T(8,128)S(1)}, f32[2,128,128]{2,1,0:T(8,128)S(1)}, u32[]{:S(2)}, u32[]{:S(2)}) collective-permute-start(f32[2,128,128]{2,1,0:T(8,128)S(1)} %multiply_add_fusion.10), channel_id=1, source_target_pairs={{0,32},{32,64},{64,96},{96,128},{128,160},{160,192},{192,224},{224... | collective-permute-start | bytes 393224 | tf_op jit(solution)/shard_map/while/body/eval_jaxpr/ppermute | solution.py:13
  42.3 8.1 %collective-permute-start = (f32[2,128,128]{2,1,0:T(8,128)S(1)}, f32[2,128,128]{2,1,0:T(8,128)S(1)}, u32[]{:S(2)}, u32[]{:S(2)}) collective-permute-start(f32[2,128,128]{2,1,0:T(8,128)S(1)} %multiply_add_fusion.10), channel_id=1, source_target_pairs={{0,32},{32,64},{64,96},{96,128},{128,160},{160,192},{192,224},{224... | collective-permute-start | bytes 393224 | tf_op jit(solution)/shard_map/while/body/eval_jaxpr/ppermute | solution.py:13
  50.5 9.0 %collective-permute-start = (f32[2,128,128]{2,1,0:T(8,128)S(1)}, f32[2,128,128]{2,1,0:T(8,128)S(1)}, u32[]{:S(2)}, u32[]{:S(2)}) collective-permute-start(f32[2,128,128]{2,1,0:T(8,128)S(1)} %multiply_add_fusion.10), channel_id=1, source_target_pairs={{0,32},{32,64},{64,96},{96,128},{128,160},{160,192},{192,224},{224... | collective-permute-start | bytes 393224 | tf_op jit(solution)/shard_map/while/body/eval_jaxpr/ppermute | solution.py:13
  59.6 8.7 %collective-permute-start = (f32[2,128,128]{2,1,0:T(8,128)S(1)}, f32[2,128,128]{2,1,0:T(8,128)S(1)}, u32[]{:S(2)}, u32[]{:S(2)}) collective-permute-start(f32[2,128,128]{2,1,0:T(8,128)S(1)} %multiply_add_fusion.10), channel_id=1, source_target_pairs={{0,32},{32,64},{64,96},{96,128},{128,160},{160,192},{192,224},{224... | collective-permute-start | bytes 393224 | tf_op jit(solution)/shard_map/while/body/eval_jaxpr/ppermute | solution.py:13
  68.4 8.1 %collective-permute-start = (f32[2,128,128]{2,1,0:T(8,128)S(1)}, f32[2,128,128]{2,1,0:T(8,128)S(1)}, u32[]{:S(2)}, u32[]{:S(2)}) collective-permute-start(f32[2,128,128]{2,1,0:T(8,128)S(1)} %multiply_add_fusion.10), channel_id=1, source_target_pairs={{0,32},{32,64},{64,96},{96,128},{128,160},{160,192},{192,224},{224... | collective-permute-start | bytes 393224 | tf_op jit(solution)/shard_map/while/body/eval_jaxpr/ppermute | solution.py:13
  76.6 8.1 %collective-permute-start = (f32[2,128,128]{2,1,0:T(8,128)S(1)}, f32[2,128,128]{2,1,0:T(8,128)S(1)}, u32[]{:S(2)}, u32[]{:S(2)}) collective-permute-start(f32[2,128,128]{2,1,0:T(8,128)S(1)} %multiply_add_fusion.10), channel_id=1, source_target_pairs={{0,32},{32,64},{64,96},{96,128},{128,160},{160,192},{192,224},{224... | collective-permute-start | bytes 393224 | tf_op jit(solution)/shard_map/while/body/eval_jaxpr/ppermute | solution.py:13
  84.8 8.1 %collective-permute-start = (f32[2,128,128]{2,1,0:T(8,128)S(1)}, f32[2,128,128]{2,1,0:T(8,128)S(1)}, u32[]{:S(2)}, u32[]{:S(2)}) collective-permute-start(f32[2,128,128]{2,1,0:T(8,128)S(1)} %multiply_add_fusion.10), channel_id=1, source_target_pairs={{0,32},{32,64},{64,96},{96,128},{128,160},{160,192},{192,224},{224... | collective-permute-start | bytes 393224 | tf_op jit(solution)/shard_map/while/body/eval_jaxpr/ppermute | solution.py:13
  92.9 8.1 %collective-permute-start = (f32[2,128,128]{2,1,0:T(8,128)S(1)}, f32[2,128,128]{2,1,0:T(8,128)S(1)}, u32[]{:S(2)}, u32[]{:S(2)}) collective-permute-start(f32[2,128,128]{2,1,0:T(8,128)S(1)} %multiply_add_fusion.10), channel_id=1, source_target_pairs={{0,32},{32,64},{64,96},{96,128},{128,160},{160,192},{192,224},{224... | collective-permute-start | bytes 393224 | tf_op jit(solution)/shard_map/while/body/eval_jaxpr/ppermute | solution.py:13
  101.1 8.6 %collective-permute-start = (f32[2,128,128]{2,1,0:T(8,128)S(1)}, f32[2,128,128]{2,1,0:T(8,128)S(1)}, u32[]{:S(2)}, u32[]{:S(2)}) collective-permute-start(f32[2,128,128]{2,1,0:T(8,128)S(1)} %multiply_add_fusion.10), channel_id=1, source_target_pairs={{0,32},{32,64},{64,96},{96,128},{128,160},{160,192},{192,224},{224... | collective-permute-start | bytes 393224 | tf_op jit(solution)/shard_map/while/body/eval_jaxpr/ppermute | solution.py:13
  109.8 9.2 %collective-permute-start = (f32[2,128,128]{2,1,0:T(8,128)S(1)}, f32[2,128,128]{2,1,0:T(8,128)S(1)}, u32[]{:S(2)}, u32[]{:S(2)}) collective-permute-start(f32[2,128,128]{2,1,0:T(8,128)S(1)} %multiply_add_fusion.10), channel_id=1, source_target_pairs={{0,32},{32,64},{64,96},{96,128},{128,160},{160,192},{192,224},{224... | collective-permute-start | bytes 393224 | tf_op jit(solution)/shard_map/while/body/eval_jaxpr/ppermute | solution.py:13
  119.0 8.1 %collective-permute-start = (f32[2,128,128]{2,1,0:T(8,128)S(1)}, f32[2,128,128]{2,1,0:T(8,128)S(1)}, u32[]{:S(2)}, u32[]{:S(2)}) collective-permute-start(f32[2,128,128]{2,1,0:T(8,128)S(1)} %multiply_add_fusion.10), channel_id=1, source_target_pairs={{0,32},{32,64},{64,96},{96,128},{128,160},{160,192},{192,224},{224... | collective-permute-start | bytes 393224 | tf_op jit(solution)/shard_map/while/body/eval_jaxpr/ppermute | solution.py:13
  127.2 8.1 %collective-permute-start = (f32[2,128,128]{2,1,0:T(8,128)S(1)}, f32[2,128,128]{2,1,0:T(8,128)S(1)}, u32[]{:S(2)}, u32[]{:S(2)}) collective-permute-start(f32[2,128,128]{2,1,0:T(8,128)S(1)} %multiply_add_fusion.10), channel_id=1, source_target_pairs={{0,32},{32,64},{64,96},{96,128},{128,160},{160,192},{192,224},{224... | collective-permute-start | bytes 393224 | tf_op jit(solution)/shard_map/while/body/eval_jaxpr/ppermute | solution.py:13
  135.3 1.4 copy-start.13
  135.4 2.7 copy-start.2
  135.4 2.7 copy-start.4
  135.4 2.7 copy-start.6
  136.7 3.2 copy-start
  138.2 66.0 %copy-start.1 = (bf16[1024,256]{1,0:T(8,128)(2,1)S(1)}, bf16[1024,256]{1,0:T(8,128)(2,1)}, u32[]{:S(2)}) copy-start(bf16[1024,256]{1,0:T(8,128)(2,1)} %param.15) | copy-start | bytes 1572868
  138.2 66.0 %copy-start.22 = (f32[256]{0:T(256)S(1)}, f32[256]{0:T(256)}, u32[]{:S(2)}) copy-start(f32[256]{0:T(256)} %param.14) | copy-start | bytes 3076
  303.1 6.1 %copy-start.14 = (f32[2,4,256]{2,1,0:T(4,128)S(1)}, f32[2,4,256]{2,1,0:T(4,128)}, u32[]{:S(2)}) copy-start(f32[2,4,256]{2,1,0:T(4,128)} %get-tuple-element.137) | copy-start | bytes 24580
  309.1 1.2 copy-start.16
  309.1 1.3 copy-start.18
  309.1 1.3 copy-start.21
  309.1 1.3 copy-start.23
  312.1 8.6 %collective-permute-start.1 = (f32[2,128,128]{2,1,0:T(8,128)}, f32[2,128,128]{2,1,0:T(8,128)S(1)}, u32[]{:S(2)}, u32[]{:S(2)}) collective-permute-start(f32[2,128,128]{2,1,0:T(8,128)} %multiply_add_fusion.11), channel_id=1, source_target_pairs={{32,0},{64,32},{96,64},{128,96},{160,128},{192,160},{224,192},{256... | collective-permute-start | bytes 393224 | tf_op jit(solution)/shard_map/while/body/eval_jaxpr/ppermute | solution.py:13
  322.1 8.3 %collective-permute-start.1 = (f32[2,128,128]{2,1,0:T(8,128)}, f32[2,128,128]{2,1,0:T(8,128)S(1)}, u32[]{:S(2)}, u32[]{:S(2)}) collective-permute-start(f32[2,128,128]{2,1,0:T(8,128)} %multiply_add_fusion.11), channel_id=1, source_target_pairs={{32,0},{64,32},{96,64},{128,96},{160,128},{192,160},{224,192},{256... | collective-permute-start | bytes 393224 | tf_op jit(solution)/shard_map/while/body/eval_jaxpr/ppermute | solution.py:13
  331.8 8.3 %collective-permute-start.1 = (f32[2,128,128]{2,1,0:T(8,128)}, f32[2,128,128]{2,1,0:T(8,128)S(1)}, u32[]{:S(2)}, u32[]{:S(2)}) collective-permute-start(f32[2,128,128]{2,1,0:T(8,128)} %multiply_add_fusion.11), channel_id=1, source_target_pairs={{32,0},{64,32},{96,64},{128,96},{160,128},{192,160},{224,192},{256... | collective-permute-start | bytes 393224 | tf_op jit(solution)/shard_map/while/body/eval_jaxpr/ppermute | solution.py:13
  341.5 8.3 %collective-permute-start.1 = (f32[2,128,128]{2,1,0:T(8,128)}, f32[2,128,128]{2,1,0:T(8,128)S(1)}, u32[]{:S(2)}, u32[]{:S(2)}) collective-permute-start(f32[2,128,128]{2,1,0:T(8,128)} %multiply_add_fusion.11), channel_id=1, source_target_pairs={{32,0},{64,32},{96,64},{128,96},{160,128},{192,160},{224,192},{256... | collective-permute-start | bytes 393224 | tf_op jit(solution)/shard_map/while/body/eval_jaxpr/ppermute | solution.py:13
  351.2 8.3 %collective-permute-start.1 = (f32[2,128,128]{2,1,0:T(8,128)}, f32[2,128,128]{2,1,0:T(8,128)S(1)}, u32[]{:S(2)}, u32[]{:S(2)}) collective-permute-start(f32[2,128,128]{2,1,0:T(8,128)} %multiply_add_fusion.11), channel_id=1, source_target_pairs={{32,0},{64,32},{96,64},{128,96},{160,128},{192,160},{224,192},{256... | collective-permute-start | bytes 393224 | tf_op jit(solution)/shard_map/while/body/eval_jaxpr/ppermute | solution.py:13
  360.8 8.3 %collective-permute-start.1 = (f32[2,128,128]{2,1,0:T(8,128)}, f32[2,128,128]{2,1,0:T(8,128)S(1)}, u32[]{:S(2)}, u32[]{:S(2)}) collective-permute-start(f32[2,128,128]{2,1,0:T(8,128)} %multiply_add_fusion.11), channel_id=1, source_target_pairs={{32,0},{64,32},{96,64},{128,96},{160,128},{192,160},{224,192},{256... | collective-permute-start | bytes 393224 | tf_op jit(solution)/shard_map/while/body/eval_jaxpr/ppermute | solution.py:13
  370.5 8.9 %collective-permute-start.1 = (f32[2,128,128]{2,1,0:T(8,128)}, f32[2,128,128]{2,1,0:T(8,128)S(1)}, u32[]{:S(2)}, u32[]{:S(2)}) collective-permute-start(f32[2,128,128]{2,1,0:T(8,128)} %multiply_add_fusion.11), channel_id=1, source_target_pairs={{32,0},{64,32},{96,64},{128,96},{160,128},{192,160},{224,192},{256... | collective-permute-start | bytes 393224 | tf_op jit(solution)/shard_map/while/body/eval_jaxpr/ppermute | solution.py:13
  380.8 9.3 %collective-permute-start.1 = (f32[2,128,128]{2,1,0:T(8,128)}, f32[2,128,128]{2,1,0:T(8,128)S(1)}, u32[]{:S(2)}, u32[]{:S(2)}) collective-permute-start(f32[2,128,128]{2,1,0:T(8,128)} %multiply_add_fusion.11), channel_id=1, source_target_pairs={{32,0},{64,32},{96,64},{128,96},{160,128},{192,160},{224,192},{256... | collective-permute-start | bytes 393224 | tf_op jit(solution)/shard_map/while/body/eval_jaxpr/ppermute | solution.py:13
  391.5 8.5 %collective-permute-start.1 = (f32[2,128,128]{2,1,0:T(8,128)}, f32[2,128,128]{2,1,0:T(8,128)S(1)}, u32[]{:S(2)}, u32[]{:S(2)}) collective-permute-start(f32[2,128,128]{2,1,0:T(8,128)} %multiply_add_fusion.11), channel_id=1, source_target_pairs={{32,0},{64,32},{96,64},{128,96},{160,128},{192,160},{224,192},{256... | collective-permute-start | bytes 393224 | tf_op jit(solution)/shard_map/while/body/eval_jaxpr/ppermute | solution.py:13
  401.4 8.3 %collective-permute-start.1 = (f32[2,128,128]{2,1,0:T(8,128)}, f32[2,128,128]{2,1,0:T(8,128)S(1)}, u32[]{:S(2)}, u32[]{:S(2)}) collective-permute-start(f32[2,128,128]{2,1,0:T(8,128)} %multiply_add_fusion.11), channel_id=1, source_target_pairs={{32,0},{64,32},{96,64},{128,96},{160,128},{192,160},{224,192},{256... | collective-permute-start | bytes 393224 | tf_op jit(solution)/shard_map/while/body/eval_jaxpr/ppermute | solution.py:13
  411.1 8.3 %collective-permute-start.1 = (f32[2,128,128]{2,1,0:T(8,128)}, f32[2,128,128]{2,1,0:T(8,128)S(1)}, u32[]{:S(2)}, u32[]{:S(2)}) collective-permute-start(f32[2,128,128]{2,1,0:T(8,128)} %multiply_add_fusion.11), channel_id=1, source_target_pairs={{32,0},{64,32},{96,64},{128,96},{160,128},{192,160},{224,192},{256... | collective-permute-start | bytes 393224 | tf_op jit(solution)/shard_map/while/body/eval_jaxpr/ppermute | solution.py:13
  420.8 8.3 %collective-permute-start.1 = (f32[2,128,128]{2,1,0:T(8,128)}, f32[2,128,128]{2,1,0:T(8,128)S(1)}, u32[]{:S(2)}, u32[]{:S(2)}) collective-permute-start(f32[2,128,128]{2,1,0:T(8,128)} %multiply_add_fusion.11), channel_id=1, source_target_pairs={{32,0},{64,32},{96,64},{128,96},{160,128},{192,160},{224,192},{256... | collective-permute-start | bytes 393224 | tf_op jit(solution)/shard_map/while/body/eval_jaxpr/ppermute | solution.py:13
  430.5 8.3 %collective-permute-start.1 = (f32[2,128,128]{2,1,0:T(8,128)}, f32[2,128,128]{2,1,0:T(8,128)S(1)}, u32[]{:S(2)}, u32[]{:S(2)}) collective-permute-start(f32[2,128,128]{2,1,0:T(8,128)} %multiply_add_fusion.11), channel_id=1, source_target_pairs={{32,0},{64,32},{96,64},{128,96},{160,128},{192,160},{224,192},{256... | collective-permute-start | bytes 393224 | tf_op jit(solution)/shard_map/while/body/eval_jaxpr/ppermute | solution.py:13
  440.1 8.3 %collective-permute-start.1 = (f32[2,128,128]{2,1,0:T(8,128)}, f32[2,128,128]{2,1,0:T(8,128)S(1)}, u32[]{:S(2)}, u32[]{:S(2)}) collective-permute-start(f32[2,128,128]{2,1,0:T(8,128)} %multiply_add_fusion.11), channel_id=1, source_target_pairs={{32,0},{64,32},{96,64},{128,96},{160,128},{192,160},{224,192},{256... | collective-permute-start | bytes 393224 | tf_op jit(solution)/shard_map/while/body/eval_jaxpr/ppermute | solution.py:13
  449.8 8.3 %collective-permute-start.1 = (f32[2,128,128]{2,1,0:T(8,128)}, f32[2,128,128]{2,1,0:T(8,128)S(1)}, u32[]{:S(2)}, u32[]{:S(2)}) collective-permute-start(f32[2,128,128]{2,1,0:T(8,128)} %multiply_add_fusion.11), channel_id=1, source_target_pairs={{32,0},{64,32},{96,64},{128,96},{160,128},{192,160},{224,192},{256... | collective-permute-start | bytes 393224 | tf_op jit(solution)/shard_map/while/body/eval_jaxpr/ppermute | solution.py:13
  458.8 3.3 copy-start.10
  463.5 1.9 copy-start.12
  466.1 1.4 copy-start.3
  466.1 1.4 copy-start.5
  466.1 1.4 copy-start.7
where the time goes:
time: 473 us; the launch traced here: 471 us
  blocking collectives  158 us (33%)
  waiting for transfers between devices  138 us (29%)
  starting transfers between devices  112 us (24%)
  other arithmetic  29.4 us (6%)
  matrix products  20.7 us (4%)
  local copies, waits for them, and re-layouts  11.8 us (2%)
    ppermute x30, waiting for transfers between devices, passed_along(): lax.ppermute(value, axis, [(source, source + steps) for source in range(i...  138 us
    ppermute x30, starting transfers between devices, passed_along(): lax.ppermute(value, axis, [(source, source + steps) for source in range(i...  112 us
    psum x1, blocking collectives, local(): squares = lax.psum(jnp.sum(flattened * flattened, axis=1), 'head')  62.7 us
    psum x1, blocking collectives, local(): projected = lax.psum(jnp.sum(normed_grad * normed, axis=1), 'head')  62.7 us
    psum x1, blocking collectives, local(): gain_grad = lax.psum(gain_part, 'seq')  32.4 us
    add x15, other arithmetic, relay_step(): outgoing = jnp.exp(device_decay)[:, None, None] * suffix + device_back  21.1 us
  transfers between devices with their start and end apart: 30, of which 30 were waited for; matrix products, arithmetic and copies ran while one was open for 0% of the time, Pallas kernels for 0%

commit v1 on v0

--- a/solution.py
+++ b/solution.py
@@ -130,7 +130,11 @@
     value_grad = value_grad + to_end * jnp.einsum(
         "hnjd,hnde->hnje", key_blocks, leaving, precision=highest
     )
-    gain_grad = lax.psum(gain_part, "seq")
+    n_dev = lax.axis_size("seq")
+    gain_grad, hop = (gain_part, 1)
+    while hop < n_dev:
+        gain_grad = gain_grad + lax.ppermute(gain_grad, "seq", [(i, i ^ hop) for i in range(n_dev)])
+        hop = 2 * hop
     return (
         output,
         from_blocks(query_grad).astype(jnp.bfloat16),

time: 473 us -> 462 us (0.977)
  blocking collectives: 158 us -> 126 us
  starting transfers between devices: 112 us -> 133 us
  other arithmetic: 29.4 us -> 22.7 us
  waiting for transfers between devices: 138 us -> 143 us
    psum x1 -> x0, blocking collectives: 32.4 us -> none  [local(): gain_grad = lax.psum(gain_part, 'seq')]
    ppermute x0 -> x4, starting transfers between devices: none -> 19.3 us  [local(): lax.ppermute(gain_grad, 'seq', [(i, i ^ hop) for i in range(n_dev)])]
    add x15, other arithmetic: 21.1 us -> 10.6 us  [relay_step(): outgoing = jnp.exp(device_decay)[:, None, None] * suffix + device_back]
  transfers between devices with their start and end apart: 30 -> 34, of which waited for: 30 -> 31; matrix products, arithmetic and copies ran while one was open for 0% -> 8% of each run, Pallas kernels for 0% -> 0%
where the time goes in v1:
time: 462 us; the launch traced here: 460 us
  waiting for transfers between devices  143 us (31%)
  starting transfers between devices  133 us (29%)
  blocking collectives  126 us (27%)
  other arithmetic  22.7 us (5%)
  matrix products  21.2 us (5%)
  local copies, waits for them, and re-layouts  12.3 us (3%)
    ppermute x30, waiting for transfers between devices, passed_along(): lax.ppermute(value, axis, [(source, source + steps) for source in range(i...  139 us
    ppermute x30, starting transfers between devices, passed_along(): lax.ppermute(value, axis, [(source, source + steps) for source in range(i...  114 us
    psum x1, blocking collectives, local(): projected = lax.psum(jnp.sum(normed_grad * normed, axis=1), 'head')  63.7 us
    psum x1, blocking collectives, local(): squares = lax.psum(jnp.sum(flattened * flattened, axis=1), 'head')  62.7 us
    ppermute x4, starting transfers between devices, local(): lax.ppermute(gain_grad, 'seq', [(i, i ^ hop) for i in range(n_dev)])  19.3 us
    add x15, other arithmetic, relay_step(): outgoing = jnp.exp(device_decay)[:, None, None] * suffix + device_back  10.6 us
  transfers between devices with their start and end apart: 34, of which 31 were waited for; matrix products, arithmetic and copies ran while one was open for 8% of the time, Pallas kernels for 0%

profile of v1, /device:TPU:96, one launch (start us, length us, event | category | flops | bytes accessed | tf_op | source)
XLA Modules:
  0.0 460.1 jit_solution(8078839543657161149)
XLA Ops:
  1.3 2.4 reduce-window.6
  9.8 125.4 %while.24 = (s32[]{:T(128)}, f32[2,128,128]{2,1,0:T(8,128)S(1)}, f32[2,1,1]{0,2,1:T(1,128)S(1)}, f32[2,128,128]{2,1,0:T(8,128)S(1)}, s32[]{:T(128)}) while((s32[]{:T(128)}, f32[2,128,128]{2,1,0:T(8,128)S(1)}, f32[2,1,1]{0,2,1:T(1,128)S(1)}, f32[2,128,128]{2,1,0:T(8,128)S(1)}, s32[]{:T(128)}) %tuple.63), condition=%wide.region_4.5_spmd, body=%wide.region_3.4_spmd.sunk | while | flops 65538 | bytes 917613 | solution.py:32
  9.9 5.0 %collective-permute-start = (f32[2,128,128]{2,1,0:T(8,128)S(1)}, f32[2,128,128]{2,1,0:T(8,128)S(1)}, u32[]{:S(2)}, u32[]{:S(2)}) collective-permute-start(f32[2,128,128]{2,1,0:T(8,128)S(1)} %multiply_add_fusion.10), channel_id=1, source_target_pairs={{0,32},{32,64},{64,96},{96,128},{128,160},{160,192},{192,224},{224... | collective-permute-start | bytes 393224 | tf_op jit(solution)/shard_map/while/body/eval_jaxpr/ppermute | solution.py:13
  14.9 2.7 collective-permute-done
  17.8 5.6 %collective-permute-start = (f32[2,128,128]{2,1,0:T(8,128)S(1)}, f32[2,128,128]{2,1,0:T(8,128)S(1)}, u32[]{:S(2)}, u32[]{:S(2)}) collective-permute-start(f32[2,128,128]{2,1,0:T(8,128)S(1)} %multiply_add_fusion.10), channel_id=1, source_target_pairs={{0,32},{32,64},{64,96},{96,128},{128,160},{160,192},{192,224},{224... | collective-permute-start | bytes 393224 | tf_op jit(solution)/shard_map/while/body/eval_jaxpr/ppermute | solution.py:13
  23.4 2.5 collective-permute-done
  25.9 5.6 %collective-permute-start = (f32[2,128,128]{2,1,0:T(8,128)S(1)}, f32[2,128,128]{2,1,0:T(8,128)S(1)}, u32[]{:S(2)}, u32[]{:S(2)}) collective-permute-start(f32[2,128,128]{2,1,0:T(8,128)S(1)} %multiply_add_fusion.10), channel_id=1, source_target_pairs={{0,32},{32,64},{64,96},{96,128},{128,160},{160,192},{192,224},{224... | collective-permute-start | bytes 393224 | tf_op jit(solution)/shard_map/while/body/eval_jaxpr/ppermute | solution.py:13
  31.5 2.5 collective-permute-done
  34.1 5.6 %collective-permute-start = (f32[2,128,128]{2,1,0:T(8,128)S(1)}, f32[2,128,128]{2,1,0:T(8,128)S(1)}, u32[]{:S(2)}, u32[]{:S(2)}) collective-permute-start(f32[2,128,128]{2,1,0:T(8,128)S(1)} %multiply_add_fusion.10), channel_id=1, source_target_pairs={{0,32},{32,64},{64,96},{96,128},{128,160},{160,192},{192,224},{224... | collective-permute-start | bytes 393224 | tf_op jit(solution)/shard_map/while/body/eval_jaxpr/ppermute | solution.py:13
  39.7 2.5 collective-permute-done
  42.3 5.6 %collective-permute-start = (f32[2,128,128]{2,1,0:T(8,128)S(1)}, f32[2,128,128]{2,1,0:T(8,128)S(1)}, u32[]{:S(2)}, u32[]{:S(2)}) collective-permute-start(f32[2,128,128]{2,1,0:T(8,128)S(1)} %multiply_add_fusion.10), channel_id=1, source_target_pairs={{0,32},{32,64},{64,96},{96,128},{128,160},{160,192},{192,224},{224... | collective-permute-start | bytes 393224 | tf_op jit(solution)/shard_map/while/body/eval_jaxpr/ppermute | solution.py:13
  47.8 2.5 collective-permute-done
  50.4 5.6 %collective-permute-start = (f32[2,128,128]{2,1,0:T(8,128)S(1)}, f32[2,128,128]{2,1,0:T(8,128)S(1)}, u32[]{:S(2)}, u32[]{:S(2)}) collective-permute-start(f32[2,128,128]{2,1,0:T(8,128)S(1)} %multiply_add_fusion.10), channel_id=1, source_target_pairs={{0,32},{32,64},{64,96},{96,128},{128,160},{160,192},{192,224},{224... | collective-permute-start | bytes 393224 | tf_op jit(solution)/shard_map/while/body/eval_jaxpr/ppermute | solution.py:13
  56.0 3.4 collective-permute-done
  59.5 5.6 %collective-permute-start = (f32[2,128,128]{2,1,0:T(8,128)S(1)}, f32[2,128,128]{2,1,0:T(8,128)S(1)}, u32[]{:S(2)}, u32[]{:S(2)}) collective-permute-start(f32[2,128,128]{2,1,0:T(8,128)S(1)} %multiply_add_fusion.10), channel_id=1, source_target_pairs={{0,32},{32,64},{64,96},{96,128},{128,160},{160,192},{192,224},{224... | collective-permute-start | bytes 393224 | tf_op jit(solution)/shard_map/while/body/eval_jaxpr/ppermute | solution.py:13
  65.1 3.1 collective-permute-done
  68.3 5.6 %collective-permute-start = (f32[2,128,128]{2,1,0:T(8,128)S(1)}, f32[2,128,128]{2,1,0:T(8,128)S(1)}, u32[]{:S(2)}, u32[]{:S(2)}) collective-permute-start(f32[2,128,128]{2,1,0:T(8,128)S(1)} %multiply_add_fusion.10), channel_id=1, source_target_pairs={{0,32},{32,64},{64,96},{96,128},{128,160},{160,192},{192,224},{224... | collective-permute-start | bytes 393224 | tf_op jit(solution)/shard_map/while/body/eval_jaxpr/ppermute | solution.py:13
  74.0 2.5 collective-permute-done
  76.5 5.6 %collective-permute-start = (f32[2,128,128]{2,1,0:T(8,128)S(1)}, f32[2,128,128]{2,1,0:T(8,128)S(1)}, u32[]{:S(2)}, u32[]{:S(2)}) collective-permute-start(f32[2,128,128]{2,1,0:T(8,128)S(1)} %multiply_add_fusion.10), channel_id=1, source_target_pairs={{0,32},{32,64},{64,96},{96,128},{128,160},{160,192},{192,224},{224... | collective-permute-start | bytes 393224 | tf_op jit(solution)/shard_map/while/body/eval_jaxpr/ppermute | solution.py:13
  82.1 2.5 collective-permute-done
  84.7 5.6 %collective-permute-start = (f32[2,128,128]{2,1,0:T(8,128)S(1)}, f32[2,128,128]{2,1,0:T(8,128)S(1)}, u32[]{:S(2)}, u32[]{:S(2)}) collective-permute-start(f32[2,128,128]{2,1,0:T(8,128)S(1)} %multiply_add_fusion.10), channel_id=1, source_target_pairs={{0,32},{32,64},{64,96},{96,128},{128,160},{160,192},{192,224},{224... | collective-permute-start | bytes 393224 | tf_op jit(solution)/shard_map/while/body/eval_jaxpr/ppermute | solution.py:13
  90.3 2.5 collective-permute-done
  92.9 5.6 %collective-permute-start = (f32[2,128,128]{2,1,0:T(8,128)S(1)}, f32[2,128,128]{2,1,0:T(8,128)S(1)}, u32[]{:S(2)}, u32[]{:S(2)}) collective-permute-start(f32[2,128,128]{2,1,0:T(8,128)S(1)} %multiply_add_fusion.10), channel_id=1, source_target_pairs={{0,32},{32,64},{64,96},{96,128},{128,160},{160,192},{192,224},{224... | collective-permute-start | bytes 393224 | tf_op jit(solution)/shard_map/while/body/eval_jaxpr/ppermute | solution.py:13
  98.4 2.5 collective-permute-done
  101.0 5.6 %collective-permute-start = (f32[2,128,128]{2,1,0:T(8,128)S(1)}, f32[2,128,128]{2,1,0:T(8,128)S(1)}, u32[]{:S(2)}, u32[]{:S(2)}) collective-permute-start(f32[2,128,128]{2,1,0:T(8,128)S(1)} %multiply_add_fusion.10), channel_id=1, source_target_pairs={{0,32},{32,64},{64,96},{96,128},{128,160},{160,192},{192,224},{224... | collective-permute-start | bytes 393224 | tf_op jit(solution)/shard_map/while/body/eval_jaxpr/ppermute | solution.py:13
  106.6 3.0 collective-permute-done
  109.7 5.6 %collective-permute-start = (f32[2,128,128]{2,1,0:T(8,128)S(1)}, f32[2,128,128]{2,1,0:T(8,128)S(1)}, u32[]{:S(2)}, u32[]{:S(2)}) collective-permute-start(f32[2,128,128]{2,1,0:T(8,128)S(1)} %multiply_add_fusion.10), channel_id=1, source_target_pairs={{0,32},{32,64},{64,96},{96,128},{128,160},{160,192},{192,224},{224... | collective-permute-start | bytes 393224 | tf_op jit(solution)/shard_map/while/body/eval_jaxpr/ppermute | solution.py:13
  115.3 3.5 collective-permute-done
  118.9 5.6 %collective-permute-start = (f32[2,128,128]{2,1,0:T(8,128)S(1)}, f32[2,128,128]{2,1,0:T(8,128)S(1)}, u32[]{:S(2)}, u32[]{:S(2)}) collective-permute-start(f32[2,128,128]{2,1,0:T(8,128)S(1)} %multiply_add_fusion.10), channel_id=1, source_target_pairs={{0,32},{32,64},{64,96},{96,128},{128,160},{160,192},{192,224},{224... | collective-permute-start | bytes 393224 | tf_op jit(solution)/shard_map/while/body/eval_jaxpr/ppermute | solution.py:13
  124.6 2.5 collective-permute-done
  127.1 5.6 %collective-permute-start = (f32[2,128,128]{2,1,0:T(8,128)S(1)}, f32[2,128,128]{2,1,0:T(8,128)S(1)}, u32[]{:S(2)}, u32[]{:S(2)}) collective-permute-start(f32[2,128,128]{2,1,0:T(8,128)S(1)} %multiply_add_fusion.10), channel_id=1, source_target_pairs={{0,32},{32,64},{64,96},{96,128},{128,160},{160,192},{192,224},{224... | collective-permute-start | bytes 393224 | tf_op jit(solution)/shard_map/while/body/eval_jaxpr/ppermute | solution.py:13
  132.7 2.5 collective-permute-done
  140.3 62.7 %psum.14 = f32[1024]{0:T(1024)S(1)} all-reduce(f32[1024]{0:T(1024)S(1)} %bitcast.231), channel_id=1, replica_groups=mesh['seq'=16,'head'=32] {'head'}, use_global_device_ids=true, to_apply=%region_6.7 | all-reduce | flops 1024 | bytes 8192 | tf_op jit(solution)/shard_map/psum | solution.py:92
  208.9 63.7 %psum.15 = f32[1024]{0:T(1024)} all-reduce(f32[1024]{0:T(1024)} %get-tuple-element.108), channel_id=1, replica_groups=mesh['seq'=16,'head'=32] {'head'}, use_global_device_ids=true, to_apply=%region_8.9 | all-reduce | flops 1024 | bytes 8192 | tf_op jit(solution)/shard_map/psum | solution.py:95
  273.3 2.2 fusion.16
  277.2 6.1 %convolution_bitcast_fusion.4 = f32[4,256,2,128]{3,1,0,2:T(8,128)} fusion(f32[2,4,256,256]{3,2,1,0:T(8,128)} %copy-done, f32[4,256,2,128]{3,2,1,0:T(2,128)S(1)} %reshape.129), kind=kOutput, calls=%fused_computation.11 | convolution fusion | flops 805306368 | bytes 4194304 | tf_op jit(solution)/shard_map/hnij,hnid->hnjd/dot_general | solution.py:108
  284.6 2.9 convolution_bitcast_fusion
  294.9 139.3 %while.25 = (s32[]{:T(128)}, f32[2,128,128]{2,1,0:T(8,128)S(1)}, f32[2,1,1]{0,2,1:T(1,128)}, f32[2,128,128]{2,1,0:T(8,128)S(1)}, s32[]{:T(128)}) while((s32[]{:T(128)}, f32[2,128,128]{2,1,0:T(8,128)S(1)}, f32[2,1,1]{0,2,1:T(1,128)}, f32[2,128,128]{2,1,0:T(8,128)S(1)}, s32[]{:T(128)}) %tuple.69), condition=%wide.region_10.11_spmd, body=%wide.region_9.10_spmd.sunk | while | flops 65538 | bytes 917613 | solution.py:41
  295.7 3.8 collective-permute-start.1
  299.5 9.5 %collective-permute-done.1 = f32[2,128,128]{2,1,0:T(8,128)S(1)} collective-permute-done((f32[2,128,128]{2,1,0:T(8,128)S(1)}, f32[2,128,128]{2,1,0:T(8,128)S(1)}, u32[]{:S(2)}, u32[]{:S(2)}) %collective-permute-start.1) | collective-permute-done | bytes 131104 | tf_op jit(solution)/shard_map/while/body/eval_jaxpr/ppermute | solution.py:13
  309.7 1.9 collective-permute-start.1
  311.6 6.1 %collective-permute-done.1 = f32[2,128,128]{2,1,0:T(8,128)S(1)} collective-permute-done((f32[2,128,128]{2,1,0:T(8,128)S(1)}, f32[2,128,128]{2,1,0:T(8,128)S(1)}, u32[]{:S(2)}, u32[]{:S(2)}) %collective-permute-start.1) | collective-permute-done | bytes 131104 | tf_op jit(solution)/shard_map/while/body/eval_jaxpr/ppermute | solution.py:13
  318.5 1.9 collective-permute-start.1
  320.4 6.1 %collective-permute-done.1 = f32[2,128,128]{2,1,0:T(8,128)S(1)} collective-permute-done((f32[2,128,128]{2,1,0:T(8,128)S(1)}, f32[2,128,128]{2,1,0:T(8,128)S(1)}, u32[]{:S(2)}, u32[]{:S(2)}) %collective-permute-start.1) | collective-permute-done | bytes 131104 | tf_op jit(solution)/shard_map/while/body/eval_jaxpr/ppermute | solution.py:13
  329.2 6.1 %collective-permute-done.1 = f32[2,128,128]{2,1,0:T(8,128)S(1)} collective-permute-done((f32[2,128,128]{2,1,0:T(8,128)S(1)}, f32[2,128,128]{2,1,0:T(8,128)S(1)}, u32[]{:S(2)}, u32[]{:S(2)}) %collective-permute-start.1) | collective-permute-done | bytes 131104 | tf_op jit(solution)/shard_map/while/body/eval_jaxpr/ppermute | solution.py:13
  336.0 1.9 collective-permute-start.1
  338.0 6.1 %collective-permute-done.1 = f32[2,128,128]{2,1,0:T(8,128)S(1)} collective-permute-done((f32[2,128,128]{2,1,0:T(8,128)S(1)}, f32[2,128,128]{2,1,0:T(8,128)S(1)}, u32[]{:S(2)}, u32[]{:S(2)}) %collective-permute-start.1) | collective-permute-done | bytes 131104 | tf_op jit(solution)/shard_map/while/body/eval_jaxpr/ppermute | solution.py:13
  346.8 6.5 %collective-permute-done.1 = f32[2,128,128]{2,1,0:T(8,128)S(1)} collective-permute-done((f32[2,128,128]{2,1,0:T(8,128)S(1)}, f32[2,128,128]{2,1,0:T(8,128)S(1)}, u32[]{:S(2)}, u32[]{:S(2)}) %collective-permute-start.1) | collective-permute-done | bytes 131104 | tf_op jit(solution)/shard_map/while/body/eval_jaxpr/ppermute | solution.py:13
  353.9 1.9 collective-permute-start.1
  355.9 7.5 %collective-permute-done.1 = f32[2,128,128]{2,1,0:T(8,128)S(1)} collective-permute-done((f32[2,128,128]{2,1,0:T(8,128)S(1)}, f32[2,128,128]{2,1,0:T(8,128)S(1)}, u32[]{:S(2)}, u32[]{:S(2)}) %collective-permute-start.1) | collective-permute-done | bytes 131104 | tf_op jit(solution)/shard_map/while/body/eval_jaxpr/ppermute | solution.py:13
  366.0 6.6 %collective-permute-done.1 = f32[2,128,128]{2,1,0:T(8,128)S(1)} collective-permute-done((f32[2,128,128]{2,1,0:T(8,128)S(1)}, f32[2,128,128]{2,1,0:T(8,128)S(1)}, u32[]{:S(2)}, u32[]{:S(2)}) %collective-permute-start.1) | collective-permute-done | bytes 131104 | tf_op jit(solution)/shard_map/while/body/eval_jaxpr/ppermute | solution.py:13
  375.2 6.1 %collective-permute-done.1 = f32[2,128,128]{2,1,0:T(8,128)S(1)} collective-permute-done((f32[2,128,128]{2,1,0:T(8,128)S(1)}, f32[2,128,128]{2,1,0:T(8,128)S(1)}, u32[]{:S(2)}, u32[]{:S(2)}) %collective-permute-start.1) | collective-permute-done | bytes 131104 | tf_op jit(solution)/shard_map/while/body/eval_jaxpr/ppermute | solution.py:13
  382.1 1.9 collective-permute-start.1
  384.0 6.1 %collective-permute-done.1 = f32[2,128,128]{2,1,0:T(8,128)S(1)} collective-permute-done((f32[2,128,128]{2,1,0:T(8,128)S(1)}, f32[2,128,128]{2,1,0:T(8,128)S(1)}, u32[]{:S(2)}, u32[]{:S(2)}) %collective-permute-start.1) | collective-permute-done | bytes 131104 | tf_op jit(solution)/shard_map/while/body/eval_jaxpr/ppermute | solution.py:13
  392.8 6.1 %collective-permute-done.1 = f32[2,128,128]{2,1,0:T(8,128)S(1)} collective-permute-done((f32[2,128,128]{2,1,0:T(8,128)S(1)}, f32[2,128,128]{2,1,0:T(8,128)S(1)}, u32[]{:S(2)}, u32[]{:S(2)}) %collective-permute-start.1) | collective-permute-done | bytes 131104 | tf_op jit(solution)/shard_map/while/body/eval_jaxpr/ppermute | solution.py:13
  401.6 6.1 %collective-permute-done.1 = f32[2,128,128]{2,1,0:T(8,128)S(1)} collective-permute-done((f32[2,128,128]{2,1,0:T(8,128)S(1)}, f32[2,128,128]{2,1,0:T(8,128)S(1)}, u32[]{:S(2)}, u32[]{:S(2)}) %collective-permute-start.1) | collective-permute-done | bytes 131104 | tf_op jit(solution)/shard_map/while/body/eval_jaxpr/ppermute | solution.py:13
  408.4 1.9 collective-permute-start.1
  410.3 6.3 %collective-permute-done.1 = f32[2,128,128]{2,1,0:T(8,128)S(1)} collective-permute-done((f32[2,128,128]{2,1,0:T(8,128)S(1)}, f32[2,128,128]{2,1,0:T(8,128)S(1)}, u32[]{:S(2)}, u32[]{:S(2)}) %collective-permute-start.1) | collective-permute-done | bytes 131104 | tf_op jit(solution)/shard_map/while/body/eval_jaxpr/ppermute | solution.py:13
  417.4 1.9 collective-permute-start.1
  419.3 6.1 %collective-permute-done.1 = f32[2,128,128]{2,1,0:T(8,128)S(1)} collective-permute-done((f32[2,128,128]{2,1,0:T(8,128)S(1)}, f32[2,128,128]{2,1,0:T(8,128)S(1)}, u32[]{:S(2)}, u32[]{:S(2)}) %collective-permute-start.1) | collective-permute-done | bytes 131104 | tf_op jit(solution)/shard_map/while/body/eval_jaxpr/ppermute | solution.py:13
  428.1 6.1 %collective-permute-done.1 = f32[2,128,128]{2,1,0:T(8,128)S(1)} collective-permute-done((f32[2,128,128]{2,1,0:T(8,128)S(1)}, f32[2,128,128]{2,1,0:T(8,128)S(1)}, u32[]{:S(2)}, u32[]{:S(2)}) %collective-permute-start.1) | collective-permute-done | bytes 131104 | tf_op jit(solution)/shard_map/while/body/eval_jaxpr/ppermute | solution.py:13
  434.4 4.7 %collective-permute-start.4 = (f32[256]{0:T(256)S(1)}, f32[256]{0:T(256)S(1)}, u32[]{:S(2)}, u32[]{:S(2)}) collective-permute-start(f32[256]{0:T(256)S(1)} %add.121), channel_id=1, source_target_pairs={{0,128},{32,160},{64,192},{96,224},{128,0},{160,32},{192,64},{224,... | collective-permute-start | bytes 3080 | tf_op jit(solution)/shard_map/ppermute | solution.py:136
  439.7 4.1 collective-permute-done.4
  443.9 10.8 %collective-permute-start.5 = (f32[256]{0:T(256)S(1)}, f32[256]{0:T(256)S(1)}, u32[]{:S(2)}, u32[]{:S(2)}) collective-permute-start(f32[256]{0:T(256)S(1)} %add.122), channel_id=1, source_target_pairs={{0,256},{32,288},{64,320},{96,352},{128,384},{160,416},{192,448},{... | collective-permute-start | bytes 3080 | tf_op jit(solution)/shard_map/ppermute | solution.py:136
  (143 shorter events, 60.0 us)
Async XLA Ops:
  4.7 4.9 %copy-start.20 = (f32[2]{0:T(128)}, f32[2]{0:T(128)S(1)}, u32[]{:S(2)}) copy-start(f32[2]{0:T(128)S(1)} %get-tuple-element.109) | copy-start | bytes 28
  4.7 130.5 %copy-start.14 = (f32[2]{0:T(128)}, f32[2]{0:T(128)S(1)}, u32[]{:S(2)}) copy-start(f32[2]{0:T(128)S(1)} %get-tuple-element.111) | copy-start | bytes 28
  4.7 130.5 %copy-start.17 = (f32[2]{0:T(128)}, f32[2]{0:T(128)S(1)}, u32[]{:S(2)}) copy-start(f32[2]{0:T(128)S(1)} %get-tuple-element.112) | copy-start | bytes 28
  4.7 130.5 %copy-start.22 = (f32[2]{0:T(128)}, f32[2]{0:T(128)S(1)}, u32[]{:S(2)}) copy-start(f32[2]{0:T(128)S(1)} %get-tuple-element.110) | copy-start | bytes 28
  5.4 131.0 %copy-start.8 = (pred[256,256]{1,0:T(8,128)(4,1)}, pred[256,256]{1,0:T(8,128)(4,1)S(1)}, u32[]{:S(2)}) copy-start(pred[256,256]{1,0:T(8,128)(4,1)S(1)} %iota_compare_fusion) | copy-start | bytes 196612
  9.6 126.2 %copy-start.7 = (bf16[1024,256]{1,0:T(8,128)(2,1)S(1)}, bf16[1024,256]{1,0:T(8,128)(2,1)}, u32[]{:S(2)}) copy-start(bf16[1024,256]{1,0:T(8,128)(2,1)} %param.10) | copy-start | bytes 1572868
  9.9 7.8 %collective-permute-start = (f32[2,128,128]{2,1,0:T(8,128)S(1)}, f32[2,128,128]{2,1,0:T(8,128)S(1)}, u32[]{:S(2)}, u32[]{:S(2)}) collective-permute-start(f32[2,128,128]{2,1,0:T(8,128)S(1)} %multiply_add_fusion.10), channel_id=1, source_target_pairs={{0,32},{32,64},{64,96},{96,128},{128,160},{160,192},{192,224},{224... | collective-permute-start | bytes 393224 | tf_op jit(solution)/shard_map/while/body/eval_jaxpr/ppermute | solution.py:13
  17.8 8.1 %collective-permute-start = (f32[2,128,128]{2,1,0:T(8,128)S(1)}, f32[2,128,128]{2,1,0:T(8,128)S(1)}, u32[]{:S(2)}, u32[]{:S(2)}) collective-permute-start(f32[2,128,128]{2,1,0:T(8,128)S(1)} %multiply_add_fusion.10), channel_id=1, source_target_pairs={{0,32},{32,64},{64,96},{96,128},{128,160},{160,192},{192,224},{224... | collective-permute-start | bytes 393224 | tf_op jit(solution)/shard_map/while/body/eval_jaxpr/ppermute | solution.py:13
  25.9 8.1 %collective-permute-start = (f32[2,128,128]{2,1,0:T(8,128)S(1)}, f32[2,128,128]{2,1,0:T(8,128)S(1)}, u32[]{:S(2)}, u32[]{:S(2)}) collective-permute-start(f32[2,128,128]{2,1,0:T(8,128)S(1)} %multiply_add_fusion.10), channel_id=1, source_target_pairs={{0,32},{32,64},{64,96},{96,128},{128,160},{160,192},{192,224},{224... | collective-permute-start | bytes 393224 | tf_op jit(solution)/shard_map/while/body/eval_jaxpr/ppermute | solution.py:13
  34.1 8.1 %collective-permute-start = (f32[2,128,128]{2,1,0:T(8,128)S(1)}, f32[2,128,128]{2,1,0:T(8,128)S(1)}, u32[]{:S(2)}, u32[]{:S(2)}) collective-permute-start(f32[2,128,128]{2,1,0:T(8,128)S(1)} %multiply_add_fusion.10), channel_id=1, source_target_pairs={{0,32},{32,64},{64,96},{96,128},{128,160},{160,192},{192,224},{224... | collective-permute-start | bytes 393224 | tf_op jit(solution)/shard_map/while/body/eval_jaxpr/ppermute | solution.py:13
  42.3 8.1 %collective-permute-start = (f32[2,128,128]{2,1,0:T(8,128)S(1)}, f32[2,128,128]{2,1,0:T(8,128)S(1)}, u32[]{:S(2)}, u32[]{:S(2)}) collective-permute-start(f32[2,128,128]{2,1,0:T(8,128)S(1)} %multiply_add_fusion.10), channel_id=1, source_target_pairs={{0,32},{32,64},{64,96},{96,128},{128,160},{160,192},{192,224},{224... | collective-permute-start | bytes 393224 | tf_op jit(solution)/shard_map/while/body/eval_jaxpr/ppermute | solution.py:13
  50.4 9.0 %collective-permute-start = (f32[2,128,128]{2,1,0:T(8,128)S(1)}, f32[2,128,128]{2,1,0:T(8,128)S(1)}, u32[]{:S(2)}, u32[]{:S(2)}) collective-permute-start(f32[2,128,128]{2,1,0:T(8,128)S(1)} %multiply_add_fusion.10), channel_id=1, source_target_pairs={{0,32},{32,64},{64,96},{96,128},{128,160},{160,192},{192,224},{224... | collective-permute-start | bytes 393224 | tf_op jit(solution)/shard_map/while/body/eval_jaxpr/ppermute | solution.py:13
  59.5 8.7 %collective-permute-start = (f32[2,128,128]{2,1,0:T(8,128)S(1)}, f32[2,128,128]{2,1,0:T(8,128)S(1)}, u32[]{:S(2)}, u32[]{:S(2)}) collective-permute-start(f32[2,128,128]{2,1,0:T(8,128)S(1)} %multiply_add_fusion.10), channel_id=1, source_target_pairs={{0,32},{32,64},{64,96},{96,128},{128,160},{160,192},{192,224},{224... | collective-permute-start | bytes 393224 | tf_op jit(solution)/shard_map/while/body/eval_jaxpr/ppermute | solution.py:13
  68.3 8.1 %collective-permute-start = (f32[2,128,128]{2,1,0:T(8,128)S(1)}, f32[2,128,128]{2,1,0:T(8,128)S(1)}, u32[]{:S(2)}, u32[]{:S(2)}) collective-permute-start(f32[2,128,128]{2,1,0:T(8,128)S(1)} %multiply_add_fusion.10), channel_id=1, source_target_pairs={{0,32},{32,64},{64,96},{96,128},{128,160},{160,192},{192,224},{224... | collective-permute-start | bytes 393224 | tf_op jit(solution)/shard_map/while/body/eval_jaxpr/ppermute | solution.py:13
  76.5 8.1 %collective-permute-start = (f32[2,128,128]{2,1,0:T(8,128)S(1)}, f32[2,128,128]{2,1,0:T(8,128)S(1)}, u32[]{:S(2)}, u32[]{:S(2)}) collective-permute-start(f32[2,128,128]{2,1,0:T(8,128)S(1)} %multiply_add_fusion.10), channel_id=1, source_target_pairs={{0,32},{32,64},{64,96},{96,128},{128,160},{160,192},{192,224},{224... | collective-permute-start | bytes 393224 | tf_op jit(solution)/shard_map/while/body/eval_jaxpr/ppermute | solution.py:13
  84.7 8.1 %collective-permute-start = (f32[2,128,128]{2,1,0:T(8,128)S(1)}, f32[2,128,128]{2,1,0:T(8,128)S(1)}, u32[]{:S(2)}, u32[]{:S(2)}) collective-permute-start(f32[2,128,128]{2,1,0:T(8,128)S(1)} %multiply_add_fusion.10), channel_id=1, source_target_pairs={{0,32},{32,64},{64,96},{96,128},{128,160},{160,192},{192,224},{224... | collective-permute-start | bytes 393224 | tf_op jit(solution)/shard_map/while/body/eval_jaxpr/ppermute | solution.py:13
  92.9 8.1 %collective-permute-start = (f32[2,128,128]{2,1,0:T(8,128)S(1)}, f32[2,128,128]{2,1,0:T(8,128)S(1)}, u32[]{:S(2)}, u32[]{:S(2)}) collective-permute-start(f32[2,128,128]{2,1,0:T(8,128)S(1)} %multiply_add_fusion.10), channel_id=1, source_target_pairs={{0,32},{32,64},{64,96},{96,128},{128,160},{160,192},{192,224},{224... | collective-permute-start | bytes 393224 | tf_op jit(solution)/shard_map/while/body/eval_jaxpr/ppermute | solution.py:13
  101.0 8.6 %collective-permute-start = (f32[2,128,128]{2,1,0:T(8,128)S(1)}, f32[2,128,128]{2,1,0:T(8,128)S(1)}, u32[]{:S(2)}, u32[]{:S(2)}) collective-permute-start(f32[2,128,128]{2,1,0:T(8,128)S(1)} %multiply_add_fusion.10), channel_id=1, source_target_pairs={{0,32},{32,64},{64,96},{96,128},{128,160},{160,192},{192,224},{224... | collective-permute-start | bytes 393224 | tf_op jit(solution)/shard_map/while/body/eval_jaxpr/ppermute | solution.py:13
  109.7 9.2 %collective-permute-start = (f32[2,128,128]{2,1,0:T(8,128)S(1)}, f32[2,128,128]{2,1,0:T(8,128)S(1)}, u32[]{:S(2)}, u32[]{:S(2)}) collective-permute-start(f32[2,128,128]{2,1,0:T(8,128)S(1)} %multiply_add_fusion.10), channel_id=1, source_target_pairs={{0,32},{32,64},{64,96},{96,128},{128,160},{160,192},{192,224},{224... | collective-permute-start | bytes 393224 | tf_op jit(solution)/shard_map/while/body/eval_jaxpr/ppermute | solution.py:13
  118.9 8.1 %collective-permute-start = (f32[2,128,128]{2,1,0:T(8,128)S(1)}, f32[2,128,128]{2,1,0:T(8,128)S(1)}, u32[]{:S(2)}, u32[]{:S(2)}) collective-permute-start(f32[2,128,128]{2,1,0:T(8,128)S(1)} %multiply_add_fusion.10), channel_id=1, source_target_pairs={{0,32},{32,64},{64,96},{96,128},{128,160},{160,192},{192,224},{224... | collective-permute-start | bytes 393224 | tf_op jit(solution)/shard_map/while/body/eval_jaxpr/ppermute | solution.py:13
  127.1 8.1 %collective-permute-start = (f32[2,128,128]{2,1,0:T(8,128)S(1)}, f32[2,128,128]{2,1,0:T(8,128)S(1)}, u32[]{:S(2)}, u32[]{:S(2)}) collective-permute-start(f32[2,128,128]{2,1,0:T(8,128)S(1)} %multiply_add_fusion.10), channel_id=1, source_target_pairs={{0,32},{32,64},{64,96},{96,128},{128,160},{160,192},{192,224},{224... | collective-permute-start | bytes 393224 | tf_op jit(solution)/shard_map/while/body/eval_jaxpr/ppermute | solution.py:13
  135.2 0.5 copy-start.12
  135.9 2.7 copy-start.5
  137.1 3.2 copy-start
  137.1 1.4 copy-start.10
  138.6 66.6 %copy-start.3 = (bf16[1024,256]{1,0:T(8,128)(2,1)S(1)}, bf16[1024,256]{1,0:T(8,128)(2,1)}, u32[]{:S(2)}) copy-start(bf16[1024,256]{1,0:T(8,128)(2,1)} %param.15) | copy-start | bytes 1572868
  207.0 85.3 %collective-permute-start.2 = (f32[256]{0:T(256)}, f32[256]{0:T(256)}, u32[]{:S(2)}, u32[]{:S(2)}) collective-permute-start(f32[256]{0:T(256)} %get-tuple-element.107), channel_id=1, source_target_pairs={{0,32},{32,0},{64,96},{96,64},{128,160},{160,128},{192,224},{224,1... | collective-permute-start | bytes 3080 | tf_op jit(solution)/shard_map/ppermute | solution.py:136
  277.2 6.1 %copy-start.9 = (pred[256,256]{1,0:T(8,128)(4,1)S(1)}, pred[256,256]{1,0:T(8,128)(4,1)}, u32[]{:S(2)}) copy-start(pred[256,256]{1,0:T(8,128)(4,1)} %copy-done.8) | copy-start | bytes 196612
  287.5 1.4 copy-start.13
  287.5 2.6 copy-start.6
  287.5 2.6 copy-start.11
  290.1 2.0 copy-start.15
  290.1 2.0 copy-start.18
  290.1 2.0 copy-start.23
  290.1 2.0 copy-start.24
  292.1 142.1 %copy-start.16 = (f32[2]{0:T(128)S(1)}, f32[2]{0:T(128)}, u32[]{:S(2)}) copy-start(f32[2]{0:T(128)} %copy-done.14) | copy-start | bytes 28
  292.1 142.1 %copy-start.19 = (f32[2]{0:T(128)S(1)}, f32[2]{0:T(128)}, u32[]{:S(2)}) copy-start(f32[2]{0:T(128)} %copy-done.17) | copy-start | bytes 28
  292.1 142.2 %copy-start.21 = (f32[2]{0:T(128)S(1)}, f32[2]{0:T(128)}, u32[]{:S(2)}) copy-start(f32[2]{0:T(128)} %copy-done.20) | copy-start | bytes 28
  292.1 147.0 %copy-start.2 = (f32[4,256,2,128]{3,1,0,2:T(8,128)S(1)}, f32[4,256,2,128]{3,1,0,2:T(8,128)}, u32[]{:S(2)}) copy-start(f32[4,256,2,128]{3,1,0,2:T(8,128)} %convolution_bitcast_fusion.4) | copy-start | bytes 3145732
  293.0 141.3 %collective-permute-start.3 = (f32[256]{0:T(256)S(1)}, f32[256]{0:T(256)S(1)}, u32[]{:S(2)}, u32[]{:S(2)}) collective-permute-start(f32[256]{0:T(256)S(1)} %add.120), channel_id=1, source_target_pairs={{0,64},{32,96},{64,0},{96,32},{128,192},{160,224},{192,128},{224,1... | collective-permute-start | bytes 3080 | tf_op jit(solution)/shard_map/ppermute | solution.py:136
  295.7 13.3 %collective-permute-start.1 = (f32[2,128,128]{2,1,0:T(8,128)S(1)}, f32[2,128,128]{2,1,0:T(8,128)S(1)}, u32[]{:S(2)}, u32[]{:S(2)}) collective-permute-start(f32[2,128,128]{2,1,0:T(8,128)S(1)} %multiply_add_fusion.11), channel_id=1, source_target_pairs={{32,0},{64,32},{96,64},{128,96},{160,128},{192,160},{224,192},{256... | collective-permute-start | bytes 393224 | tf_op jit(solution)/shard_map/while/body/eval_jaxpr/ppermute | solution.py:13
  309.7 8.1 %collective-permute-start.1 = (f32[2,128,128]{2,1,0:T(8,128)S(1)}, f32[2,128,128]{2,1,0:T(8,128)S(1)}, u32[]{:S(2)}, u32[]{:S(2)}) collective-permute-start(f32[2,128,128]{2,1,0:T(8,128)S(1)} %multiply_add_fusion.11), channel_id=1, source_target_pairs={{32,0},{64,32},{96,64},{128,96},{160,128},{192,160},{224,192},{256... | collective-permute-start | bytes 393224 | tf_op jit(solution)/shard_map/while/body/eval_jaxpr/ppermute | solution.py:13
  318.5 8.1 %collective-permute-start.1 = (f32[2,128,128]{2,1,0:T(8,128)S(1)}, f32[2,128,128]{2,1,0:T(8,128)S(1)}, u32[]{:S(2)}, u32[]{:S(2)}) collective-permute-start(f32[2,128,128]{2,1,0:T(8,128)S(1)} %multiply_add_fusion.11), channel_id=1, source_target_pairs={{32,0},{64,32},{96,64},{128,96},{160,128},{192,160},{224,192},{256... | collective-permute-start | bytes 393224 | tf_op jit(solution)/shard_map/while/body/eval_jaxpr/ppermute | solution.py:13
  327.3 8.1 %collective-permute-start.1 = (f32[2,128,128]{2,1,0:T(8,128)S(1)}, f32[2,128,128]{2,1,0:T(8,128)S(1)}, u32[]{:S(2)}, u32[]{:S(2)}) collective-permute-start(f32[2,128,128]{2,1,0:T(8,128)S(1)} %multiply_add_fusion.11), channel_id=1, source_target_pairs={{32,0},{64,32},{96,64},{128,96},{160,128},{192,160},{224,192},{256... | collective-permute-start | bytes 393224 | tf_op jit(solution)/shard_map/while/body/eval_jaxpr/ppermute | solution.py:13
  336.0 8.1 %collective-permute-start.1 = (f32[2,128,128]{2,1,0:T(8,128)S(1)}, f32[2,128,128]{2,1,0:T(8,128)S(1)}, u32[]{:S(2)}, u32[]{:S(2)}) collective-permute-start(f32[2,128,128]{2,1,0:T(8,128)S(1)} %multiply_add_fusion.11), channel_id=1, source_target_pairs={{32,0},{64,32},{96,64},{128,96},{160,128},{192,160},{224,192},{256... | collective-permute-start | bytes 393224 | tf_op jit(solution)/shard_map/while/body/eval_jaxpr/ppermute | solution.py:13
  344.8 8.4 %collective-permute-start.1 = (f32[2,128,128]{2,1,0:T(8,128)S(1)}, f32[2,128,128]{2,1,0:T(8,128)S(1)}, u32[]{:S(2)}, u32[]{:S(2)}) collective-permute-start(f32[2,128,128]{2,1,0:T(8,128)S(1)} %multiply_add_fusion.11), channel_id=1, source_target_pairs={{32,0},{64,32},{96,64},{128,96},{160,128},{192,160},{224,192},{256... | collective-permute-start | bytes 393224 | tf_op jit(solution)/shard_map/while/body/eval_jaxpr/ppermute | solution.py:13
  353.9 9.4 %collective-permute-start.1 = (f32[2,128,128]{2,1,0:T(8,128)S(1)}, f32[2,128,128]{2,1,0:T(8,128)S(1)}, u32[]{:S(2)}, u32[]{:S(2)}) collective-permute-start(f32[2,128,128]{2,1,0:T(8,128)S(1)} %multiply_add_fusion.11), channel_id=1, source_target_pairs={{32,0},{64,32},{96,64},{128,96},{160,128},{192,160},{224,192},{256... | collective-permute-start | bytes 393224 | tf_op jit(solution)/shard_map/while/body/eval_jaxpr/ppermute | solution.py:13
  364.0 8.5 %collective-permute-start.1 = (f32[2,128,128]{2,1,0:T(8,128)S(1)}, f32[2,128,128]{2,1,0:T(8,128)S(1)}, u32[]{:S(2)}, u32[]{:S(2)}) collective-permute-start(f32[2,128,128]{2,1,0:T(8,128)S(1)} %multiply_add_fusion.11), channel_id=1, source_target_pairs={{32,0},{64,32},{96,64},{128,96},{160,128},{192,160},{224,192},{256... | collective-permute-start | bytes 393224 | tf_op jit(solution)/shard_map/while/body/eval_jaxpr/ppermute | solution.py:13
  373.3 8.1 %collective-permute-start.1 = (f32[2,128,128]{2,1,0:T(8,128)S(1)}, f32[2,128,128]{2,1,0:T(8,128)S(1)}, u32[]{:S(2)}, u32[]{:S(2)}) collective-permute-start(f32[2,128,128]{2,1,0:T(8,128)S(1)} %multiply_add_fusion.11), channel_id=1, source_target_pairs={{32,0},{64,32},{96,64},{128,96},{160,128},{192,160},{224,192},{256... | collective-permute-start | bytes 393224 | tf_op jit(solution)/shard_map/while/body/eval_jaxpr/ppermute | solution.py:13
  382.1 8.1 %collective-permute-start.1 = (f32[2,128,128]{2,1,0:T(8,128)S(1)}, f32[2,128,128]{2,1,0:T(8,128)S(1)}, u32[]{:S(2)}, u32[]{:S(2)}) collective-permute-start(f32[2,128,128]{2,1,0:T(8,128)S(1)} %multiply_add_fusion.11), channel_id=1, source_target_pairs={{32,0},{64,32},{96,64},{128,96},{160,128},{192,160},{224,192},{256... | collective-permute-start | bytes 393224 | tf_op jit(solution)/shard_map/while/body/eval_jaxpr/ppermute | solution.py:13
  390.8 8.1 %collective-permute-start.1 = (f32[2,128,128]{2,1,0:T(8,128)S(1)}, f32[2,128,128]{2,1,0:T(8,128)S(1)}, u32[]{:S(2)}, u32[]{:S(2)}) collective-permute-start(f32[2,128,128]{2,1,0:T(8,128)S(1)} %multiply_add_fusion.11), channel_id=1, source_target_pairs={{32,0},{64,32},{96,64},{128,96},{160,128},{192,160},{224,192},{256... | collective-permute-start | bytes 393224 | tf_op jit(solution)/shard_map/while/body/eval_jaxpr/ppermute | solution.py:13
  399.6 8.1 %collective-permute-start.1 = (f32[2,128,128]{2,1,0:T(8,128)S(1)}, f32[2,128,128]{2,1,0:T(8,128)S(1)}, u32[]{:S(2)}, u32[]{:S(2)}) collective-permute-start(f32[2,128,128]{2,1,0:T(8,128)S(1)} %multiply_add_fusion.11), channel_id=1, source_target_pairs={{32,0},{64,32},{96,64},{128,96},{160,128},{192,160},{224,192},{256... | collective-permute-start | bytes 393224 | tf_op jit(solution)/shard_map/while/body/eval_jaxpr/ppermute | solution.py:13
  408.4 8.2 %collective-permute-start.1 = (f32[2,128,128]{2,1,0:T(8,128)S(1)}, f32[2,128,128]{2,1,0:T(8,128)S(1)}, u32[]{:S(2)}, u32[]{:S(2)}) collective-permute-start(f32[2,128,128]{2,1,0:T(8,128)S(1)} %multiply_add_fusion.11), channel_id=1, source_target_pairs={{32,0},{64,32},{96,64},{128,96},{160,128},{192,160},{224,192},{256... | collective-permute-start | bytes 393224 | tf_op jit(solution)/shard_map/while/body/eval_jaxpr/ppermute | solution.py:13
  417.4 8.1 %collective-permute-start.1 = (f32[2,128,128]{2,1,0:T(8,128)S(1)}, f32[2,128,128]{2,1,0:T(8,128)S(1)}, u32[]{:S(2)}, u32[]{:S(2)}) collective-permute-start(f32[2,128,128]{2,1,0:T(8,128)S(1)} %multiply_add_fusion.11), channel_id=1, source_target_pairs={{32,0},{64,32},{96,64},{128,96},{160,128},{192,160},{224,192},{256... | collective-permute-start | bytes 393224 | tf_op jit(solution)/shard_map/while/body/eval_jaxpr/ppermute | solution.py:13
  426.1 8.1 %collective-permute-start.1 = (f32[2,128,128]{2,1,0:T(8,128)S(1)}, f32[2,128,128]{2,1,0:T(8,128)S(1)}, u32[]{:S(2)}, u32[]{:S(2)}) collective-permute-start(f32[2,128,128]{2,1,0:T(8,128)S(1)} %multiply_add_fusion.11), channel_id=1, source_target_pairs={{32,0},{64,32},{96,64},{128,96},{160,128},{192,160},{224,192},{256... | collective-permute-start | bytes 393224 | tf_op jit(solution)/shard_map/while/body/eval_jaxpr/ppermute | solution.py:13
  434.2 20.5 %copy-start.1 = (f32[4,256,2,128]{3,1,0,2:T(8,128)S(1)}, f32[4,256,2,128]{3,1,0,2:T(8,128)}, u32[]{:S(2)}) copy-start(f32[4,256,2,128]{3,1,0,2:T(8,128)} %convolution_bitcast_fusion) | copy-start | bytes 3145732
  434.4 9.5 %collective-permute-start.4 = (f32[256]{0:T(256)S(1)}, f32[256]{0:T(256)S(1)}, u32[]{:S(2)}, u32[]{:S(2)}) collective-permute-start(f32[256]{0:T(256)S(1)} %add.121), channel_id=1, source_target_pairs={{0,128},{32,160},{64,192},{96,224},{128,0},{160,32},{192,64},{224,... | collective-permute-start | bytes 3080 | tf_op jit(solution)/shard_map/ppermute | solution.py:136
  443.9 12.9 %copy-start.4 = (bf16[4,256,2,128]{1,3,0,2:T(8,128)(2,1)S(1)}, bf16[4,256,2,128]{1,3,0,2:T(8,128)(2,1)}, u32[]{:S(2)}) copy-start(bf16[4,256,2,128]{1,3,0,2:T(8,128)(2,1)} %fusion.12) | copy-start | bytes 1572868
  443.9 15.6 %collective-permute-start.5 = (f32[256]{0:T(256)S(1)}, f32[256]{0:T(256)S(1)}, u32[]{:S(2)}, u32[]{:S(2)}) collective-permute-start(f32[256]{0:T(256)S(1)} %add.122), channel_id=1, source_target_pairs={{0,256},{32,288},{64,320},{96,352},{128,384},{160,416},{192,448},{... | collective-permute-start | bytes 3080 | tf_op jit(solution)/shard_map/ppermute | solution.py:136
